TPU v7x, 128 devices: a whole 4x4x4 slice. The times are simulated.
128 devices in a mesh: row: 16 (over z, y), col: 8 (over x, core).
Axes of the slice: x: 4, y: 4, z: 4, core: 2. Of those that a mesh axis runs over, the one named last changes fastest.
Arguments:
- tile_values: float32 [16384, 128, 128], P(('row', 'col')), may hold values from -0.125 to 0.125
- tile_owner: int32 [16384, 1], P(('row', 'col')), may hold values from 0 to 127; in each aligned block of 128 rows (0 to 127, 128 to 255, ...) at most 2 rows name the same one
- tile_row: int32 [16384], P(('row', 'col')), may hold values from 0 to 23
- tile_col: int32 [16384], P(('row', 'col')), may hold values from 0 to 47
- tile_count: int32 [128], P(('row', 'col')), may hold values from 96 to 128, as said below
- relaxation: float32 [49152], P(('row', 'col')), may hold values from 0.3 to 1
- driving: float32 [49152, 64], P(('row', 'col')), may hold values from 0.2 to 2
- heat_weight: float32 [49152], P(('row', 'col')), may hold values from 0.1 to 3
Outputs:
- mode_flux: float32 [49152, 64], P(('row', 'col'))
- conductivity: float32 [64], replicated
Inputs may be any that keep to these rules, and one draw needn't show every extreme that they name: `tile_owner`: owner d stands for row index d // 8 and column index d % 8. Among the 128 slots of one device no owner appears more than 2 times; in some device some owner appears exactly 2 times; every owner appears somewhere. Device d's slots below tile_count[d] are used, the rest are ignored; some device uses all 128.
All inputs are finite; a program needn't handle non-finite values.
Results may differ from a plain program's by a relative error of at most 0.0001.
Values sent between devices are 32-bit elements; how exact they have to be, the bound alone decides.
A program may use at most 128 MiB of HBM per device.

v0:
```python
import functools

import jax
import jax.numpy as jnp
from jax import lax
from jax.sharding import Mesh
from jax.sharding import PartitionSpec as P

ITERS = 3
ROWT_DEV = 24
ROW = ("row_0", "row_1")
COL = ("col_0", "col_1")
ROW_COL = ("row_0", "row_1", "col_0", "col_1")


def cut_along(x, dim, devices):
    shape = x.shape
    tiles = x.reshape(*shape[:dim], devices, shape[dim] // devices, *shape[dim + 1 :])
    return jnp.moveaxis(tiles, dim, 0)


def edges_of(length, count):
    unit = 8 if length >= 8 * count else 1
    return [length // unit * k // count * unit for k in range(1, count)]


def in_order(tiles, dim):
    tiles = jnp.moveaxis(tiles, 0, dim)
    shape = tiles.shape
    return tiles.reshape(*shape[:dim], shape[dim] * shape[dim + 1], *shape[dim + 2 :])


def exchange_in_pieces(x, axis, pieces, split_dim, concat_dim):
    tiles = cut_along(x, split_dim, lax.axis_size(axis))
    cut = max(range(1, max(2, tiles.ndim - 1)), key=lambda d: tiles.shape[d])
    outs = []
    for share in jnp.split(tiles, edges_of(tiles.shape[cut], pieces), axis=cut):
        if share.size:
            outs.append(lax.all_to_all(share, axis, split_axis=0, concat_axis=0, tiled=True))
    return in_order(jnp.concatenate(outs, axis=cut), concat_dim)


def copy_for_each(x, axis):
    devices = lax.axis_size(axis)
    return lax.all_to_all(jnp.broadcast_to(x[None], (devices, *x.shape)), axis, 0, 0, tiled=True)


def gather_directly(x, axis, dim):
    tiles = copy_for_each(x, axis)
    return in_order(tiles, dim)


def sent_and_summed(x, axis, dim):
    devices = lax.axis_size(axis)
    tiles = lax.all_to_all(cut_along(x, dim, devices), axis, 0, 0, tiled=True)
    return jnp.sum(tiles, axis=0)


def one_axis_at_a_time(x, axes):
    return functools.reduce(lax.psum, axes, x)


def shards(
    tile_values, tile_owner, tile_row, tile_col, tile_count, relaxation, driving, heat_weight
):
    n_rows = lax.axis_size(ROW)
    n_cols = lax.axis_size(COL)
    devices = n_rows * n_cols
    per_device = tile_values.shape[0]
    tile_size = tile_values.shape[1]
    capacity = max(2, (2 * per_device + devices - 1) // devices)
    col_tiles = n_rows * ROWT_DEV // n_cols
    columns = driving.shape[1]
    owners = tile_owner[:, 0]
    positions = jnp.arange(per_device, dtype=jnp.int32)
    is_used = positions < tile_count[0]
    same_owner = (owners[:, None] == owners[None, :]) & (positions[None, :] < positions[:, None])
    arrival = jnp.sum(same_owner.astype(jnp.int32), axis=1)
    target = owners * capacity + arrival
    tile_code = jnp.where(is_used, tile_row * col_tiles + tile_col, -1)
    payload = jnp.zeros((devices * capacity, tile_size, tile_size), jnp.float32)
    payload = payload.at[target].set(jnp.where(is_used[:, None, None], tile_values, 0.0))
    labels = jnp.full((devices * capacity,), -1, jnp.int32).at[target].set(tile_code)
    got_values, got_labels = (
        exchange_in_pieces(payload, ROW_COL, 2, 0, 0),
        exchange_in_pieces(labels, ROW_COL, 2, 0, 0),
    )
    row_index = jnp.where(got_labels < 0, ROWT_DEV, got_labels // col_tiles)
    col_index = jnp.where(got_labels < 0, 0, got_labels % col_tiles)
    row_onehot = (jnp.arange(ROWT_DEV, dtype=jnp.int32)[:, None] == row_index[None, :]).astype(
        jnp.float32
    )
    mode_flux = relaxation[:, None] * driving
    for sweep in range(ITERS):
        panel = gather_directly(mode_flux, ROW, 0)
        picked = panel.reshape(col_tiles, tile_size, columns)[col_index]
        products = jnp.einsum("sij,sjk->sik", got_values, picked, precision=lax.Precision.HIGHEST)
        partial_sum = jnp.einsum(
            "rs,sik->rik", row_onehot, products, precision=lax.Precision.HIGHEST
        )
        partial_sum = partial_sum.reshape(ROWT_DEV * tile_size, columns)
        summed = sent_and_summed(partial_sum, COL, 0)
        mode_flux = relaxation[:, None] * (driving + summed)
    weighted_local = jnp.sum(heat_weight[:, None] * mode_flux, axis=0)
    weighted, weight_sum = (
        one_axis_at_a_time(weighted_local, ROW_COL),
        one_axis_at_a_time(jnp.sum(heat_weight), ROW_COL),
    )
    conductivity = weighted / weight_sum
    return (mode_flux, conductivity)


def solution(mesh):
    torus = Mesh(mesh.devices.reshape(4, 4, 4, 2), ("row_0", "row_1", "col_0", "col_1"))
    placed = (
        P(ROW_COL, None, None),
        P(ROW_COL, None),
        P(ROW_COL),
        P(ROW_COL),
        P(ROW_COL),
        P(ROW_COL),
        P(ROW_COL, None),
        P(ROW_COL),
    )
    return jax.shard_map(
        shards, mesh=torus, in_specs=placed, out_specs=(P(ROW_COL, None), P()), check_vma=False
    )
```

profile of v0, /device:TPU:0, one launch (start us, length us, event | category | flops | bytes accessed | tf_op | source)
XLA Modules:
  0.0 599.2 jit_solution(7974123833255168326)
XLA Ops:
  0.6 0.9 convert_reduce_fusion
  3.5 1.0 scatter_custom_fusion
  5.4 11.2 %all-to-all-start.1 = ((s32[128,1,1]{2,1,0:T(1,128)}), s32[128,1,1]{2,1,0:T(1,128)S(1)}, u32[]{:S(2)}, u32[]{:S(2)}) async-start(s32[128,1,1]{2,1,0:T(1,128)} %bitcast.5), calls=%async_computation.1 | async-start | bytes 131072 | tf_op jit(solution)/shard_map/all_to_all | solution.py:39
  16.5 0.9 broadcast_multiply_fusion
  17.5 8.4 %all-to-all-done.1 = s32[128,1,1]{2,1,0:T(1,128)S(1)} async-done(((s32[128,1,1]{2,1,0:T(1,128)}), s32[128,1,1]{2,1,0:T(1,128)S(1)}, u32[]{:S(2)}, u32[]{:S(2)}) %all-to-all-start.1) | async-done | bytes 544 | tf_op jit(solution)/shard_map/all_to_all | solution.py:39
  25.9 4.8 all-to-all-start
  30.7 9.2 %all-to-all-done = s32[128,1,1]{2,1,0:T(1,128)S(1)} async-done(((s32[128,1,1]{2,1,0:T(1,128)}), s32[128,1,1]{2,1,0:T(1,128)S(1)}, u32[]{:S(2)}, u32[]{:S(2)}) %all-to-all-start) | async-done | bytes 544 | tf_op jit(solution)/shard_map/all_to_all | solution.py:39
  39.9 1.3 broadcast_in_dim.37
  41.2 3.7 all-to-all-start.4
  44.9 7.2 %broadcast_select_fusion = f32[128,128,128]{2,1,0:T(8,128)} fusion(f32[128,128,128]{2,1,0:T(8,128)} %param.8, pred[128]{0:T(512)(128)(4,1)S(1)} %iota_compare_fusion.2), kind=kLoop, calls=%fused_computation.12 | loop fusion | flops 2097152 | bytes 16777344 | tf_op jit(solution)/shard_map/jit(_where)/select_n | solution.py:82
  52.2 7.8 %broadcast_in_dim.34 = f32[256,128,128]{2,1,0:T(8,128)} broadcast(f32[]{:T(128)} %constant.19.clone.1), dimensions={} | broadcast | bytes 16777220 | tf_op jit(solution)/shard_map/broadcast_in_dim | solution.py:81
  60.0 23.4 %scatter_fusion = f32[256,128,128]{2,1,0:T(8,128)} fusion(f32[256,128,128]{2,1,0:T(8,128)} %broadcast_in_dim.34, s32[128]{0:T(128)S(1)} %fusion.16, f32[128,128,128]{2,1,0:T(8,128)} %broadcast_select_fusion), kind=kCustom, calls=%fused_computation.4 | custom fusion | bytes 25166336 | tf_op jit(solution)/shard_map/scatter | solution.py:82
  83.4 10.9 %fusion.19 = (f32[128,2,64,128]{3,2,1,0:T(8,128)}, f32[128,2,64,128]{3,2,1,0:T(8,128)}) fusion(f32[128,2,128,128]{3,2,1,0:T(8,128)} %bitcast.43), kind=kLoop, calls=%fused_computation.45 | loop fusion | bytes 33554432 | tf_op jit(solution)/shard_map/split | solution.py:37
  94.3 106.2 %all_to_all.64 = f32[128,2,64,128]{3,2,1,0:T(8,128)} all-to-all(f32[128,2,64,128]{3,2,1,0:T(8,128)} %get-tuple-element.13), channel_id=1, replica_groups=mesh['row_0'=4,'row_1'=4,'col_0'=4,'col_1'=2] {'row_0','row_1','col_0','..., dimensions={0} | all-to-all | bytes 16777216 | tf_op jit(solution)/shard_map/all_to_all | solution.py:39
  200.6 6.2 %all-to-all-start.2 = ((f32[128,2,64,128]{3,2,1,0:T(8,128)}), f32[128,2,64,128]{3,2,1,0:T(8,128)}, u32[]{:S(2)}, u32[]{:S(2)}) async-start(f32[128,2,64,128]{3,2,1,0:T(8,128)} %get-tuple-element.12), calls=%async_computation.2 | async-start | bytes 16777216 | tf_op jit(solution)/shard_map/all_to_all | solution.py:39
  206.7 2.4 reduce.1
  209.1 2.4 reduce
  212.8 0.9 copy.97
  213.7 1.3 reshape_reshape.18
  215.0 1.9 copy.100
  217.0 4.3 gather_fusion
  221.3 84.4 %all-to-all-done.2 = f32[128,2,64,128]{3,2,1,0:T(8,128)} async-done(((f32[128,2,64,128]{3,2,1,0:T(8,128)}), f32[128,2,64,128]{3,2,1,0:T(8,128)}, u32[]{:S(2)}, u32[]{:S(2)}) %all-to-all-start.2) | async-done | bytes 8388640 | tf_op jit(solution)/shard_map/all_to_all | solution.py:39
  305.7 6.7 %pad_maximum_fusion = f32[128,2,128,128]{3,2,1,0:T(8,128)S(1)} fusion(f32[128,2,64,128]{3,2,1,0:T(8,128)} %all_to_all.64, f32[128,2,64,128]{3,2,1,0:T(8,128)} %all-to-all-done.2), kind=kLoop, calls=%fused_computation.5 | loop fusion | flops 4194304 | bytes 33554432 | tf_op jit(solution)/shard_map/concatenate | solution.py:40
  312.4 2.9 copy-done.1
  315.3 34.0 %fusion.21 = f32[256,128,64]{1,2,0:T(8,128)S(1)} fusion(f32[256,128,128]{2,1,0:T(8,128)S(1)} %bitcast.40, f32[256,128,64]{1,2,0:T(8,128)S(1)} %copy-done.1), kind=kOutput, calls=%fused_computation.47 | convolution fusion | flops 3221225472 | bytes 33554432 | tf_op jit(solution)/shard_map/sij,sjk->sik/dot_general | solution.py:97
  349.4 8.4 %fusion.4 = f32[24,128,64]{1,0,2:T(8,128)} fusion(f32[256,128,64]{1,2,0:T(8,128)S(1)} %fusion.21, s32[256]{0:T(256)S(1)} %fusion.15), kind=kOutput, calls=%fused_computation.10 | convolution fusion | flops 603985920 | bytes 9176064 | tf_op jit(solution)/shard_map/rs,sik->rik/dot_general | solution.py:98
  357.8 1.3 reshape_reshape.19
  359.2 16.9 %all_to_all.65 = f32[8,384,64]{1,2,0:T(8,128)S(1)} all-to-all(f32[8,384,64]{1,2,0:T(8,128)S(1)} %copy.102), channel_id=1, replica_groups=mesh['row_0'=4,'row_1'=4,'col_0'=4,'col_1'=2] {'col_0','col_1'}, dimensions={0} | all-to-all | bytes 1572864 | tf_op jit(solution)/shard_map/all_to_all | solution.py:55
  376.4 31.2 %all_to_all.66 = f32[16,384,64]{1,2,0:T(8,128)S(1)} all-to-all(f32[16,384,64]{1,2,0:T(8,128)S(1)} %broadcast_in_dim.38), channel_id=1, replica_groups=mesh['row_0'=4,'row_1'=4,'col_0'=4,'col_1'=2] {'row_0','row_1'}, dimensions={0} | all-to-all | bytes 3145728 | tf_op jit(solution)/shard_map/all_to_all | solution.py:45
  407.6 0.9 copy.103
  409.1 4.4 gather_fusion.1
  413.5 35.7 %fusion.22 = f32[256,128,64]{1,2,0:T(8,128)S(1)} fusion(f32[256,128,128]{2,1,0:T(8,128)} %bitcast.41, f32[256,128,64]{1,2,0:T(8,128)} %gather_fusion.1), kind=kOutput, calls=%fused_computation.48 | convolution fusion | flops 3221225472 | bytes 33554432 | tf_op jit(solution)/shard_map/sij,sjk->sik/dot_general | solution.py:97
  449.2 7.5 %fusion.2 = f32[24,128,64]{1,0,2:T(8,128)S(1)} fusion(f32[256,128,64]{1,2,0:T(8,128)S(1)} %fusion.22, s32[256]{0:T(256)S(1)} %fusion.15), kind=kOutput, calls=%fused_computation.8 | convolution fusion | flops 603985920 | bytes 9176064 | tf_op jit(solution)/shard_map/rs,sik->rik/dot_general | solution.py:98
  457.1 15.6 %all_to_all.67 = f32[8,384,64]{1,2,0:T(8,128)S(1)} all-to-all(f32[8,384,64]{1,2,0:T(8,128)S(1)} %copy.106), channel_id=1, replica_groups=mesh['row_0'=4,'row_1'=4,'col_0'=4,'col_1'=2] {'col_0','col_1'}, dimensions={0} | all-to-all | bytes 1572864 | tf_op jit(solution)/shard_map/all_to_all | solution.py:55
  472.9 25.6 %all_to_all.68 = f32[16,384,64]{1,2,0:T(8,128)S(1)} all-to-all(f32[16,384,64]{1,2,0:T(8,128)S(1)} %broadcast_in_dim.39), channel_id=1, replica_groups=mesh['row_0'=4,'row_1'=4,'col_0'=4,'col_1'=2] {'row_0','row_1'}, dimensions={0} | all-to-all | bytes 3145728 | tf_op jit(solution)/shard_map/all_to_all | solution.py:45
  498.5 0.9 copy.107
  500.0 4.4 gather_fusion.2
  504.4 35.8 %fusion.23 = f32[256,128,64]{1,2,0:T(8,128)S(1)} fusion(f32[256,128,128]{2,1,0:T(8,128)} %bitcast.42, f32[256,128,64]{1,2,0:T(8,128)} %gather_fusion.2), kind=kOutput, calls=%fused_computation.49 | convolution fusion | flops 3221225472 | bytes 33554432 | tf_op jit(solution)/shard_map/sij,sjk->sik/dot_general | solution.py:97
  540.2 7.5 %fusion = f32[24,128,64]{1,0,2:T(8,128)S(1)} fusion(f32[256,128,64]{1,2,0:T(8,128)S(1)} %fusion.23, s32[256]{0:T(256)S(1)} %fusion.15), kind=kOutput, calls=%fused_computation.6 | convolution fusion | flops 603985920 | bytes 9176064 | tf_op jit(solution)/shard_map/rs,sik->rik/dot_general | solution.py:98
  547.9 1.0 copy.110
  548.9 3.5 all-to-all-start.9
  553.1 12.4 %all-to-all-done.9 = f32[8,384,64]{1,2,0:T(8,128)S(1)} async-done(((f32[8,384,64]{1,2,0:T(8,128)}), f32[8,384,64]{1,2,0:T(8,128)S(1)}, u32[]{:S(2)}, u32[]{:S(2)}) %all-to-all-start.9) | async-done | bytes 786464 | tf_op jit(solution)/shard_map/all_to_all | solution.py:55
  565.6 0.8 multiply_reduce_fusion
  566.4 9.2 %all-reduce.2 = (f32[64]{0:T(128)S(1)}, f32[]{:T(128)}) all-reduce(f32[64]{0:T(128)S(1)} %get-tuple-element.10, f32[]{:T(128)} %reduce_sum.62), channel_id=1, replica_groups=mesh['row_0'=4,'row_1'=4,'col_0'=4,'col_1'=2] {'row_0'}, use_global_device_ids=true, to_apply=%region_7.8 | all-reduce | flops 65 | bytes 520 | tf_op jit(solution)/shard_map/psum | solution.py:60
  575.6 9.2 %all-reduce.1 = (f32[64]{0:T(128)S(1)}, f32[]{:T(128)}) all-reduce(f32[64]{0:T(128)S(1)} %get-tuple-element.6, f32[]{:T(128)} %get-tuple-element.7), channel_id=1, replica_groups=mesh['row_0'=4,'row_1'=4,'col_0'=4,'col_1'=2] {'row_1'}, use_global_device_ids=true, to_apply=%region_8.9 | all-reduce | flops 65 | bytes 520 | tf_op jit(solution)/shard_map/psum | solution.py:60
  584.8 9.5 %all-reduce = (f32[64]{0:T(128)S(1)}, f32[]{:T(128)}) all-reduce(f32[64]{0:T(128)S(1)} %get-tuple-element.4, f32[]{:T(128)} %get-tuple-element.5), channel_id=1, replica_groups=mesh['row_0'=4,'row_1'=4,'col_0'=4,'col_1'=2] {'col_0'}, use_global_device_ids=true, to_apply=%region_9.10 | all-reduce | flops 65 | bytes 520 | tf_op jit(solution)/shard_map/psum | solution.py:60
  594.3 3.2 all-reduce.3
  597.4 1.2 broadcast_divide_fusion.1
  (45 shorter events, 6.5 us)
Async XLA Ops:
  5.4 20.5 %all-to-all-start.1 = ((s32[128,1,1]{2,1,0:T(1,128)}), s32[128,1,1]{2,1,0:T(1,128)S(1)}, u32[]{:S(2)}, u32[]{:S(2)}) async-start(s32[128,1,1]{2,1,0:T(1,128)} %bitcast.5), calls=%async_computation.1 | async-start | bytes 131072 | tf_op jit(solution)/shard_map/all_to_all | solution.py:39
  25.9 14.1 %all-to-all-start = ((s32[128,1,1]{2,1,0:T(1,128)}), s32[128,1,1]{2,1,0:T(1,128)S(1)}, u32[]{:S(2)}, u32[]{:S(2)}) async-start(s32[128,1,1]{2,1,0:T(1,128)} %bitcast.4), calls=%async_computation | async-start | bytes 131072 | tf_op jit(solution)/shard_map/all_to_all | solution.py:39
  41.2 53.1 %all-to-all-start.4 = ((f32[16,384,64]{1,2,0:T(8,128)}), f32[16,384,64]{1,2,0:T(8,128)S(1)}, u32[]{:S(2)}, u32[]{:S(2)}) async-start(f32[16,384,64]{1,2,0:T(8,128)} %broadcast_in_dim.37), calls=%async_computation.4 | async-start | bytes 3145728 | tf_op jit(solution)/shard_map/all_to_all | solution.py:45
  200.6 105.1 %all-to-all-start.2 = ((f32[128,2,64,128]{3,2,1,0:T(8,128)}), f32[128,2,64,128]{3,2,1,0:T(8,128)}, u32[]{:S(2)}, u32[]{:S(2)}) async-start(f32[128,2,64,128]{3,2,1,0:T(8,128)} %get-tuple-element.12), calls=%async_computation.2 | async-start | bytes 16777216 | tf_op jit(solution)/shard_map/all_to_all | solution.py:39
  305.7 9.6 %copy-start.1 = (f32[256,128,64]{1,2,0:T(8,128)S(1)}, f32[256,128,64]{1,2,0:T(8,128)}, u32[]{:S(2)}) copy-start(f32[256,128,64]{1,2,0:T(8,128)} %gather_fusion) | copy-start | bytes 25165828
  312.4 36.9 %copy-start = (f32[128,2,128,128]{3,2,1,0:T(8,128)}, f32[128,2,128,128]{3,2,1,0:T(8,128)S(1)}, u32[]{:S(2)}) copy-start(f32[128,2,128,128]{3,2,1,0:T(8,128)S(1)} %pad_maximum_fusion) | copy-start | bytes 50331652
  349.3 26.9 %copy-start.2 = (f32[384,64]{0,1:T(8,128)S(1)}, f32[384,64]{0,1:T(8,128)}, u32[]{:S(2)}) copy-start(f32[384,64]{0,1:T(8,128)} %param.14) | copy-start | bytes 294916
  349.3 26.9 %copy-start.3 = (f32[384]{0:T(512)S(1)}, f32[384]{0:T(512)}, u32[]{:S(2)}) copy-start(f32[384]{0:T(512)} %param.13) | copy-start | bytes 4612
  540.2 12.3 %copy-start.4 = (f32[384]{0:T(512)S(1)}, f32[384]{0:T(512)}, u32[]{:S(2)}) copy-start(f32[384]{0:T(512)} %param.15) | copy-start | bytes 4612
  548.9 16.6 %all-to-all-start.9 = ((f32[8,384,64]{1,2,0:T(8,128)}), f32[8,384,64]{1,2,0:T(8,128)S(1)}, u32[]{:S(2)}, u32[]{:S(2)}) async-start(f32[8,384,64]{1,2,0:T(8,128)} %copy.110), calls=%async_computation.9 | async-start | bytes 1572864 | tf_op jit(solution)/shard_map/all_to_all | solution.py:55
where the time goes:
time: 606 us; the launch traced here: 599 us
  blocking collectives  227 us (37%)
  matrix products  129 us (21%)
  waiting for transfers between devices  114 us (19%)
  local copies, waits for them, and re-layouts  73 us (12%)
  starting transfers between devices  29.4 us (5%)
  other arithmetic  24.6 us (4%)
    all_to_all x1, blocking collectives, exchange_in_pieces(): lax.all_to_all(share, axis, split_axis=0, concat_axis=0, tiled=True)  106 us
    dot_general x3, matrix products, shards(): jnp.einsum('sij,sjk->sik', got_values, picked, precision=lax.Precision.HI...  106 us
    all_to_all x3, waiting for transfers between devices, exchange_in_pieces(): lax.all_to_all(share, axis, split_axis=0, concat_axis=0, tiled=True)  102 us
    all_to_all x2, blocking collectives, copy_for_each(): lax.all_to_all(jnp.broadcast_to(x[None], (devices, *x.shape)), axis, 0, 0...  56.8 us
    all_to_all x2, blocking collectives, sent_and_summed(): tiles = lax.all_to_all(cut_along(x, dim, devices), axis, 0, 0, tiled=True)  32.5 us
    psum x4, blocking collectives, one_axis_at_a_time(): return functools.reduce(lax.psum, axes, x)  31.1 us
    dot_general x3, matrix products, shards(): jnp.einsum('rs,sik->rik', row_onehot, products, precision=lax.Precision.H...  23.4 us
    scatter x1, local copies, waits for them, and re-layouts, shards(): payload.at[target].set(jnp.where(is_used[:, None, None], tile_values, 0.0))  23.4 us
  transfers between devices with their start and end apart: 5, of which 4 were waited for; matrix products, arithmetic and copies ran while one was open for 11% of the time, Pallas kernels for 0%

commit v1 on v0

v1 whole, which is shorter than its diff:
```python
import jax
import jax.numpy as jnp
from jax import lax
from jax.experimental import pallas as pl
from jax.experimental.pallas import tpu as pltpu
from jax.sharding import Mesh
from jax.sharding import PartitionSpec as P

ITERS = 3
TILE = 128
TEMPS = 64
ROWT_DEV = 24
SLOTS = 128
RING = 4
CHIPS = 64
COLORS = 3
HALF = COLORS * CHIPS
AXES = ("z", "y", "x", "core")
ORDERS = (("x", "y", "z"), ("y", "z", "x"), ("z", "x", "y"))
RECV_BASE = {2: 0, 1: 48, 0: 60}
RECV_TILES = 63
MESH = pl.DeviceIdType.MESH


def place(coords, color):
    order = ORDERS[color]
    return coords[order[0]] + 4 * coords[order[1]] + 16 * coords[order[2]]


def half_of(ref, first, tiles, h):
    if tiles == 1:
        return ref.at[pl.ds(first, 1), pl.ds((TEMPS // 2) * h, TEMPS // 2)]
    return ref.at[pl.ds(first + h * (tiles // 2), tiles // 2)]


def add_half(dst, first, src, src_first, tiles, h):
    if tiles == 1:
        rows = pl.ds((TEMPS // 2) * h, TEMPS // 2)
        dst[first, rows] = dst[first, rows] + src[src_first, rows]
        return

    @pl.loop(0, tiles // 2)
    def _(t):
        k = t + h * (tiles // 2)
        dst[first + k] = dst[first + k] + src[src_first + k]


def kernel(
    order_ref,
    xs_ref,
    first_ref,
    last_ref,
    tiles_hbm,
    driving_ref,
    relax_ref,
    heat_ref,
    flux_ref,
    cond_ref,
    stage,
    t_hi,
    t_lo,
    x_all,
    sums,
    y_own,
    y_pair,
    r_pair,
    r_ring,
    c_recv,
    stage_sem,
    ag_send,
    ag_recv,
    fw_send,
    fw_recv,
    pr_send,
    pr_recv,
    rs_send,
    rs_recv,
    c_send,
    c_recv_sem,
):
    coords = {a: lax.axis_index(a) for a in AXES}
    core = coords["core"]
    mate = {"core": 1 - core}

    def at(axis, step):
        return {axis: lax.rem(coords[axis] + step, RING)}

    barrier = pltpu.get_barrier_semaphore()
    for axis in ("x", "y", "z"):
        for step in (1, 2, 3):
            pl.semaphore_signal(barrier, inc=1, device_id=at(axis, step), device_id_type=MESH)
    pl.semaphore_signal(barrier, inc=1, device_id=mate, device_id_type=MESH)
    pl.semaphore_wait(barrier, 10)

    def remote(src, dst, ssem, rsem, device):
        return pltpu.make_async_remote_copy(
            src_ref=src, dst_ref=dst, send_sem=ssem, recv_sem=rsem, device_id=device, device_id_type=MESH
        )

    load = pltpu.make_async_copy(tiles_hbm, stage, stage_sem)
    load.start()

    own = [(c * 2 + core) * CHIPS + place(coords, c) for c in range(COLORS)]
    for c in range(COLORS):
        x_all[own[c]] = relax_ref[c] * driving_ref[c]
    sums[SLOTS] = jnp.zeros((TEMPS, TILE), jnp.float32)

    def block(c, p, step):
        order = ORDERS[c]
        base = lax.rem(coords[order[p]] + step, RING) * 4**p
        for q in range(p + 1, 3):
            base = base + coords[order[q]] * 4**q
        return base

    def split_tiles():
        load.wait()

        @pl.loop(0, SLOTS)
        def _(j):
            tile = stage[order_ref[j]]
            hi = tile.astype(jnp.bfloat16)
            t_hi[j] = hi
            t_lo[j] = (tile - hi.astype(jnp.float32)).astype(jnp.bfloat16)

    def gather(sweep):
        sends = []

        def xblock(c, p, step):
            return (c * 2 + core) * CHIPS + block(c, p, step)

        def forward(c, piece, step):
            ref = x_all.at[pl.ds(xblock(c, 2, step), 16)]
            copy = remote(ref, ref, fw_send.at[c, piece], fw_recv.at[c, piece], mate)
            copy.start()
            return copy

        forwards = []
        for p in range(3):
            n = 4**p
            copies = {}

            def send(c, way, part, step, h, n=n, p=p, copies=copies):
                ref = half_of(x_all, xblock(c, p, step), n, h)
                copy = remote(
                    ref, ref, ag_send.at[c, p, way, part], ag_recv.at[c, p, way, part], at(ORDERS[c][p], 1 + 2 * way)
                )
                copy.start()
                copies[c, way, part] = copy
                sends.append(copy)

            for c in range(COLORS):
                for part in range(2):
                    send(c, 0, part, 0, part)
                    send(c, 1, part, 0, 1 - part)
            if p == 2:
                for c in range(COLORS):
                    forwards.append(forward(c, 0, 0))
                pl.when(sweep == 0)(split_tiles)
            for c in range(COLORS):
                copies[c, 0, 0].wait_recv()
                send(c, 0, 2, 3, 0)
                copies[c, 1, 0].wait_recv()
                send(c, 1, 2, 1, 1)
            for c in range(COLORS):
                copies[c, 0, 1].wait_recv()
                copies[c, 1, 1].wait_recv()
                if p == 2:
                    forwards.append(forward(c, 1, 3))
                    forwards.append(forward(c, 2, 1))
            for c in range(COLORS):
                copies[c, 0, 2].wait_recv()
                copies[c, 1, 2].wait_recv()
                if p == 2:
                    forwards.append(forward(c, 3, 2))
        for copy in forwards:
            copy.wait_recv()
        for copy in forwards + sends:
            copy.wait_send()

    nt = (((1,), (1,)), ((), ()))

    def multiply():
        unroll = 8

        def some(g, acc):
            for u in range(unroll):
                j = g * unroll + u
                x = x_all[xs_ref[j]]
                hi = x.astype(jnp.bfloat16)
                lo = (x - hi.astype(jnp.float32)).astype(jnp.bfloat16)
                th = t_hi[j]
                prod = (
                    lax.dot_general(hi, th, nt, preferred_element_type=jnp.float32)
                    + lax.dot_general(lo, th, nt, preferred_element_type=jnp.float32)
                    + lax.dot_general(hi, t_lo[j], nt, preferred_element_type=jnp.float32)
                )
                acc = jnp.where(first_ref[j] != 0, 0.0, acc) + prod
                sums[j] = acc
            return acc

        lax.fori_loop(0, SLOTS // unroll, some, jnp.zeros((TEMPS, TILE), jnp.float32))

    def scatter():
        pair = []
        for c in range(COLORS):

            @pl.loop(0, CHIPS)
            def _(t, c=c):
                y_pair[c * CHIPS + t] = sums[last_ref[(c * 2 + 1 - core) * CHIPS + t]]

            copy = remote(
                y_pair.at[pl.ds(c * CHIPS, CHIPS)],
                r_pair.at[pl.ds(c * CHIPS, CHIPS)],
                pr_send.at[c],
                pr_recv.at[c],
                mate,
            )
            copy.start()
            pair.append(copy)
        for c in range(COLORS):

            @pl.loop(0, CHIPS)
            def _(t, c=c):
                y_own[c * CHIPS + t] = sums[last_ref[(c * 2 + core) * CHIPS + t]]

        sends = list(pair)
        for p in (2, 1, 0):
            n = 4**p
            copies = {}

            def yblock(c, step, p=p):
                return c * CHIPS + block(c, p, step)

            def recv(c, which, p=p, n=n):
                return c * RECV_TILES + RECV_BASE[p] + which * n

            def send(c, way, part, src, dst, p=p, copies=copies):
                copy = remote(
                    src, dst, rs_send.at[c, p, way, part], rs_recv.at[c, p, way, part], at(ORDERS[c][p], 1 + 2 * way)
                )
                copy.start()
                copies[c, way, part] = copy
                sends.append(copy)

            for c in range(COLORS):
                if p == 2:
                    pair[c].wait_recv()

                    @pl.loop(0, CHIPS)
                    def _(t, c=c):
                        y_own[c * CHIPS + t] = y_own[c * CHIPS + t] + r_pair[c * CHIPS + t]

                for way, near in ((0, 1), (1, 3)):
                    send(c, way, 0, half_of(y_own, yblock(c, 2), n, way), half_of(r_ring, recv(c, 2), n, way))
                    send(c, way, 1, half_of(y_own, yblock(c, near), n, 1 - way), half_of(r_ring, recv(c, way), n, 1 - way))
            for c in range(COLORS):
                for way, near in ((0, 1), (1, 3)):
                    copies[c, way, 0].wait_recv()
                    add_half(y_own, yblock(c, near), r_ring, recv(c, 2), n, way)
                    send(c, way, 2, half_of(y_own, yblock(c, near), n, way), half_of(r_ring, recv(c, way), n, way))
            for c in range(COLORS):
                for part in (1, 2):
                    for way in (0, 1):
                        copies[c, way, part].wait_recv()

                @pl.loop(0, n)
                def _(t, c=c):
                    k = yblock(c, 0) + t
                    y_own[k] = y_own[k] + (r_ring[recv(c, 0) + t] + r_ring[recv(c, 1) + t])

        for copy in sends:
            copy.wait_send()

    def sweep_once(sweep, carry):
        gather(sweep)
        multiply()
        scatter()
        for c in range(COLORS):
            flux = relax_ref[c] * (driving_ref[c] + y_own[c * CHIPS + place(coords, c)])
            flux_ref[c] = flux
            x_all[own[c]] = flux
        return carry

    lax.fori_loop(0, ITERS, sweep_once, 0)

    part = heat_ref[0] * flux_ref[0] + heat_ref[1] * flux_ref[1] + heat_ref[2] * flux_ref[2]
    weight = heat_ref[0] + heat_ref[1] + heat_ref[2]
    total = jnp.concatenate([part, jnp.broadcast_to(weight, (8, TILE))], axis=0)
    copies = []
    for s, axis in enumerate(("core", "x", "y", "z")):
        size = 2 if axis == "core" else RING
        here = coords[axis]
        c_recv[s * RING + here] = total
        stage_copies = []
        for step in range(1, size):
            peer = {axis: lax.rem(here + step, size)}
            ref = c_recv.at[s * RING + here]
            copy = remote(ref, ref, c_send.at[s, step - 1], c_recv_sem.at[s, step - 1], peer)
            copy.start()
            stage_copies.append(copy)
        for copy in stage_copies:
            copy.wait_recv()
        copies += stage_copies
        total = c_recv[s * RING] + c_recv[s * RING + 1]
        if size == RING:
            total = total + (c_recv[s * RING + 2] + c_recv[s * RING + 3])
    for copy in copies:
        copy.wait_send()
    sums_out = jnp.sum(total, axis=1, keepdims=True)
    cond_ref[...] = jnp.broadcast_to(sums_out[:TEMPS] / sums_out[TEMPS : TEMPS + 1], (TEMPS, TILE))


def index_of(device, color):
    coords = {"z": device // 32, "y": device // 8 % 4, "x": device // 2 % 4}
    spot = jnp.where(color == 0, place(coords, 0), jnp.where(color == 1, place(coords, 1), place(coords, 2)))
    return (color * 2 + device % 2) * CHIPS + spot


def shards(tile_values, tile_owner, tile_row, tile_col, tile_count, relaxation, driving, heat_weight):
    owner = tile_owner[:, 0]
    slots = jnp.arange(SLOTS, dtype=jnp.int32)
    is_used = slots < tile_count[0]
    row = (owner // 8) * ROWT_DEV + tile_row
    key = jnp.where(is_used, index_of(row // COLORS, row % COLORS), 2 * HALF)
    xs = index_of((tile_col // COLORS) * 8 + owner % 8, tile_col % COLORS)
    before = (key[None, :] < key[:, None]) | ((key[None, :] == key[:, None]) & (slots[None, :] < slots[:, None]))
    rank = jnp.sum(before.astype(jnp.int32), axis=1)
    is_here = (rank[None, :] == slots[:, None]).astype(jnp.int32)
    order = jnp.sum(is_here * slots[None, :], axis=1)
    xs = jnp.sum(is_here * xs[None, :], axis=1)
    keys = jnp.sum(is_here * key[None, :], axis=1)
    first = (keys != jnp.concatenate([jnp.full((1,), -1, jnp.int32), keys[:-1]])).astype(jnp.int32)
    rows = jnp.arange(2 * HALF, dtype=jnp.int32)
    upto = jnp.sum((key[None, :] <= rows[:, None]).astype(jnp.int32), axis=1)
    has = jnp.any(key[None, :] == rows[:, None], axis=1)
    last = jnp.where(has, upto - 1, SLOTS)

    smem = pl.BlockSpec(memory_space=pltpu.SMEM)
    vmem = pl.BlockSpec(memory_space=pltpu.VMEM)
    f32 = jnp.float32
    dma = pltpu.SemaphoreType.DMA
    flux, cond = pl.pallas_call(
        kernel,
        out_shape=(
            jax.ShapeDtypeStruct((COLORS, TEMPS, TILE), f32),
            jax.ShapeDtypeStruct((TEMPS, TILE), f32),
        ),
        in_specs=[smem] * 4 + [pl.BlockSpec(memory_space=pl.ANY)] + [vmem] * 3,
        out_specs=(vmem, vmem),
        scratch_shapes=[
            pltpu.VMEM((SLOTS, TILE, TILE), f32),
            pltpu.VMEM((SLOTS, TILE, TILE), jnp.bfloat16),
            pltpu.VMEM((SLOTS, TILE, TILE), jnp.bfloat16),
            pltpu.VMEM((2 * HALF, TEMPS, TILE), f32),
            pltpu.VMEM((SLOTS + 1, TEMPS, TILE), f32),
            pltpu.VMEM((HALF, TEMPS, TILE), f32),
            pltpu.VMEM((HALF, TEMPS, TILE), f32),
            pltpu.VMEM((HALF, TEMPS, TILE), f32),
            pltpu.VMEM((COLORS * RECV_TILES, TEMPS, TILE), f32),
            pltpu.VMEM((4 * RING, TEMPS + 8, TILE), f32),
            dma,
            dma((COLORS, 3, 2, 3)),
            dma((COLORS, 3, 2, 3)),
            dma((COLORS, 4)),
            dma((COLORS, 4)),
            dma((COLORS,)),
            dma((COLORS,)),
            dma((COLORS, 3, 2, 3)),
            dma((COLORS, 3, 2, 3)),
            dma((4, 3)),
            dma((4, 3)),
        ],
        compiler_params=pltpu.CompilerParams(
            collective_id=0, has_side_effects=True, vmem_limit_bytes=67043328
        ),
        name="solve",
    )(
        order,
        xs,
        first,
        last,
        tile_values,
        driving.reshape(COLORS, TILE, TEMPS).transpose(0, 2, 1),
        relaxation.reshape(COLORS, 1, TILE),
        heat_weight.reshape(COLORS, 1, TILE),
    )
    mode_flux = flux.transpose(0, 2, 1).reshape(COLORS * TILE, TEMPS)
    return mode_flux, cond[:, 0]


def solution(mesh):
    torus = Mesh(mesh.devices.reshape(4, 4, 4, 2), AXES)
    placed = (
        P(AXES, None, None),
        P(AXES, None),
        P(AXES),
        P(AXES),
        P(AXES),
        P(AXES),
        P(AXES, None),
        P(AXES),
    )
    return jax.shard_map(
        shards, mesh=torus, in_specs=placed, out_specs=(P(AXES, None), P()), check_vma=False
    )
```

time: 606 us -> 308 us (0.51)
  Pallas kernels: 0 us -> 296 us
  blocking collectives: 227 us -> 0 us
  matrix products: 129 us -> 0 us
  waiting for transfers between devices: 114 us -> 0 us
  local copies, waits for them, and re-layouts: 73 us -> 6.99 us
  starting transfers between devices: 29.4 us -> 0 us
  other arithmetic: 24.6 us -> 3.15 us
    pallas_call x0 -> x1, Pallas kernels: none -> 296 us  [shards(): pl.pallas_call(kernel, out_shape=(jax.ShapeDtypeStruct((COLORS, TEMPS, TI...]
    all_to_all x5 -> x0, blocking collectives: 196 us -> none  [the longest x1 106 us: exchange_in_pieces(): lax.all_to_all(share, axis, split_axis=0, concat_axis=0, tiled=True)]
    dot_general x6 -> x0, matrix products: 129 us -> none  [the longest x3 106 us: shards(): jnp.einsum('sij,sjk->sik', got_values, picked, precision=lax.Precision.HI...]
    all_to_all x5 -> x0, waiting for transfers between devices: 114 us -> none  [the longest x3 102 us: exchange_in_pieces(): lax.all_to_all(share, axis, split_axis=0, concat_axis=0, tiled=True)]
    psum x4 -> x0, blocking collectives: 31.1 us -> none  [one_axis_at_a_time(): return functools.reduce(lax.psum, axes, x)]
    all_to_all x5 -> x0, starting transfers between devices: 29.4 us -> none  [the longest x3 22.1 us: exchange_in_pieces(): lax.all_to_all(share, axis, split_axis=0, concat_axis=0, tiled=True)]
    scatter x2 -> x0, local copies, waits for them, and re-layouts: 24.4 us -> none  [the longest x1 23.4 us: shards(): payload.at[target].set(jnp.where(is_used[:, None, None], tile_values, 0.0))]
    gather x3 -> x0, local copies, waits for them, and re-layouts: 13 us -> none  [shards(): picked = panel.reshape(col_tiles, tile_size, columns)[col_index]]
  transfers between devices with their start and end apart: 5 -> 0, of which waited for: 4 -> 0; matrix products, arithmetic and copies ran while one was open for 11% -> 0% of each run, Pallas kernels for 0% -> 0%
where the time goes in v1:
time: 308 us; the launch traced here: 307 us
  Pallas kernels  296 us (96%)
  local copies, waits for them, and re-layouts  6.99 us (2%)
  other arithmetic  3.15 us (1%)
    pallas_call x1, Pallas kernels, shards(): pl.pallas_call(kernel, out_shape=(jax.ShapeDtypeStruct((COLORS, TEMPS, TI...  296 us

profile of v1, /device:TPU:0, one launch (start us, length us, event | category | flops | bytes accessed | tf_op | source)
XLA Modules:
  0.0 307.2 jit_solution(12834932034391626852)
XLA Ops:
  1.3 0.7 fusion.7
  2.0 0.1 fusion
  2.2 0.2 convert_reduce_fusion.1
  2.3 0.7 select_reduce_fusion
  3.0 0.6 compare_convert_fusion.first_ref
  3.7 0.1 convert_reduce_fusion
  3.8 0.6 add_select_fusion.last_ref
  4.4 1.3 reshape.21.relax_ref
  5.7 1.3 reshape.22.heat_ref
  7.0 1.5 bitcast_bitcast_fusion.driving_ref
  8.5 295.7 %solve.1 = (f32[3,64,128]{2,1,0:T(8,128)}, f32[64,128]{1,0:T(8,128)}) custom-call(s32[128]{0:T(128)} %get-tuple-element.8.order_ref, s32[128]{0:T(128)} %get-tuple-element.7.xs_ref, s32[128]{0:T(128)} %compare_convert_fusion.first_ref, s32[384]{0:T(512)} %add_select_fusion.last_ref, f32[128,128,128]{2,1,0:T(8,128)} %tiles_hbm.1, ...), custom_call_target="tpu_custom_call" | custom-call | tf_op jit(solution)/shard_map/solve/pallas_call | solution.py:342
  304.2 1.5 copy_bitcast_fusion
  305.8 1.4 slice_reduce_fusion

commit v2 on v1

v2 whole, which is shorter than its diff:
```python
import jax
import jax.numpy as jnp
from jax import lax
from jax.experimental import pallas as pl
from jax.experimental.pallas import tpu as pltpu
from jax.sharding import Mesh
from jax.sharding import PartitionSpec as P

ITERS = 3
TILE = 128
TEMPS = 64
ROWT_DEV = 24
SLOTS = 128
RING = 4
CHIPS = 64
COLORS = 3
HALF = COLORS * CHIPS
AXES = ("z", "y", "x", "core")
ORDERS = (("x", "y", "z"), ("y", "z", "x"), ("z", "x", "y"))
GROUPS = (2, 1, 3, 0)
RING_TILES = 63
NT = (((1,), (1,)), ((), ()))
MESH = pl.DeviceIdType.MESH


def place(coords, color, strides):
    order = ORDERS[color]
    return coords[order[0]] + strides[0] * coords[order[1]] + strides[1] * coords[order[2]]


X_STRIDES = (4, 16)
Y_STRIDES = (16, 4)


def kernel(
    order_ref,
    xs_ref,
    first_ref,
    last_ref,
    tiles_hbm,
    driving_ref,
    relax_ref,
    heat_ref,
    flux_ref,
    cond_ref,
    stage,
    t_hi,
    t_lo,
    x_all,
    sums,
    y_own,
    y_pair,
    r_pair,
    r_ring,
    c_all,
    stage_sem,
    g1_send,
    g1_recv,
    g2_send,
    g2_recv,
    g3_send,
    g3_recv,
    fw_send,
    fw_recv,
    pr_send,
    pr_recv,
    s3_send,
    s3_recv,
    s2_send,
    s2_recv,
    s1_send,
    s1_recv,
    c_send,
    c_recv,
):
    coords = {a: lax.axis_index(a) for a in AXES}
    core = coords["core"]
    mate = {"core": 1 - core}

    def at(axis, step):
        return {axis: lax.rem(coords[axis] + step, RING)}

    def chip_row(k):
        spot = lax.rem(coords["x"] * 2 + core + k, 8)
        return {"x": spot // 2, "core": lax.rem(spot, 2)}

    peers = [at(axis, step) for axis in ("y", "z") for step in (1, 2, 3)]
    peers += [chip_row(k) for k in range(1, 8)]
    barrier = pltpu.get_barrier_semaphore()
    for peer in peers:
        pl.semaphore_signal(barrier, inc=1, device_id=peer, device_id_type=MESH)
    load = pltpu.make_async_copy(tiles_hbm, stage, stage_sem)
    load.start()

    def lanes(c):
        return slice(c * TILE, (c + 1) * TILE)

    own = [(c * 2 + core) * CHIPS + place(coords, c, X_STRIDES) for c in range(COLORS)]
    for c in range(COLORS):
        x_all[own[c]] = relax_ref[:, lanes(c)] * driving_ref[:, lanes(c)]
    sums[SLOTS] = jnp.zeros((TEMPS, TILE), jnp.float32)
    pl.semaphore_wait(barrier, len(peers))

    def along(c, p, step):
        return lax.rem(coords[ORDERS[c][p]] + step, RING)

    sends = []

    def remote(src, dst, ssem, rsem, device):
        copy = pltpu.make_async_remote_copy(
            src_ref=src, dst_ref=dst, send_sem=ssem, recv_sem=rsem, device_id=device, device_id_type=MESH
        )
        copy.start()
        sends.append(copy)
        return copy

    def drain():
        for copy in sends:
            copy.wait_send()
        sends.clear()

    def to(c, p, way):
        return at(ORDERS[c][p], 1 + 2 * way)

    def split_tiles():
        load.wait()

        @pl.loop(0, SLOTS)
        def _(j):
            tile = stage[order_ref[j]]
            hi = tile.astype(jnp.bfloat16)
            t_hi[j] = hi
            t_lo[j] = (tile - hi.astype(jnp.float32)).astype(jnp.bfloat16)

    everyone = range(COLORS)
    ways = (0, 1)

    def gather(sweep):
        near, far, wide, forwards = {}, {}, {}, []
        wide2 = {}

        def xt(c, j, g):
            return (c * 2 + core) * CHIPS + along(c, 2, j) * 16 + along(c, 1, g) * 4

        def tiles(first, count):
            return x_all.at[pl.ds(first, count)]

        def forward(c, piece, first, count):
            ref = tiles(first, count)
            forwards.append(remote(ref, ref, fw_send.at[c, piece], fw_recv.at[c, piece], mate))

        def block(c, g):
            for w in ways:
                ref = tiles(xt(c, 0, g), 4)
                wide[c, g, w] = remote(ref, ref, g3_send.at[c, g, w, 0], g3_recv.at[c, g, w, 0], to(c, 2, w))

        def relay(c, g):
            for w in ways:
                wide[c, g, w].wait_recv()
                ref = tiles(xt(c, 3 - 2 * w, g) + 2 * w, 2)
                wide2[c, g, w] = remote(ref, ref, g3_send.at[c, g, w, 1], g3_recv.at[c, g, w, 1], to(c, 2, w))
            for w in ways:
                forward(c, 1 + g * 3 + w, xt(c, 3 - 2 * w, g), 4)

        def arrived(c, g):
            for w in ways:
                wide2[c, g, w].wait_recv()
            forward(c, 3 + g * 3, xt(c, 2, g), 4)

        for c in everyone:
            for step in (1, 3, 2):
                ref = tiles(own[c], 1)
                near[c, step] = remote(
                    ref, ref, g1_send.at[c, step - 1], g1_recv.at[c, step - 1], at(ORDERS[c][0], step)
                )
        for c in everyone:
            for step in (1, 3, 2):
                near[c, step].wait_recv()
            for w in ways:
                ref = tiles(xt(c, 0, 0), 4)
                far[c, w] = remote(ref, ref, g2_send.at[c, w, 0], g2_recv.at[c, w, 0], to(c, 1, w))
        for c in everyone:
            block(c, 0)
        for c in everyone:
            for w in ways:
                far[c, w].wait_recv()
                ref = tiles(xt(c, 0, 3 - 2 * w) + 2 * w, 2)
                far[c, w] = remote(ref, ref, g2_send.at[c, w, 1], g2_recv.at[c, w, 1], to(c, 1, w))
        for g in (3, 1):
            for c in everyone:
                block(c, g)
        pl.when(sweep == 0)(split_tiles)
        for c in everyone:
            relay(c, 0)
        for c in everyone:
            for w in ways:
                far[c, w].wait_recv()
            block(c, 2)
            forward(c, 0, (c * 2 + core) * CHIPS + along(c, 2, 0) * 16, 16)
        for g in (3, 1):
            for c in everyone:
                relay(c, g)
        for c in everyone:
            arrived(c, 0)
        for c in everyone:
            relay(c, 2)
        for g in (3, 1, 2):
            for c in everyone:
                arrived(c, g)
        for copy in forwards:
            copy.wait_recv()
        drain()

    def multiply():
        unroll = 8

        def some(g, acc):
            for u in range(unroll):
                j = g * unroll + u
                x = x_all[xs_ref[j]]
                hi = x.astype(jnp.bfloat16)
                lo = (x - hi.astype(jnp.float32)).astype(jnp.bfloat16)
                both = lax.dot_general(
                    jnp.concatenate([hi, lo], axis=0), t_hi[j], NT, preferred_element_type=jnp.float32
                )
                rest = lax.dot_general(hi, t_lo[j], NT, preferred_element_type=jnp.float32)
                prod = both[:TEMPS] + both[TEMPS:] + rest
                acc = jnp.where(first_ref[j] != 0, 0.0, acc) + prod
                sums[j] = acc
            return acc

        lax.fori_loop(0, SLOTS // unroll, some, jnp.zeros((TEMPS, TILE), jnp.float32))

    def scatter():
        pair, half, full = {}, {}, {}

        def yt(c, g, j):
            return c * CHIPS + along(c, 1, g) * 16 + along(c, 2, j) * 4

        def rt(c, g):
            return c * RING_TILES + g * 12

        def give(c, g):
            first = along(c, 1, g) * 16

            @pl.loop(0, 4)
            def _(q):
                for u in range(4):
                    k = first + q * 4 + u
                    y_pair[c * CHIPS + k] = sums[last_ref[(c * 2 + 1 - core) * CHIPS + k]]

            span = pl.ds(c * CHIPS + first, 16)
            pair[c, g] = remote(y_pair.at[span], r_pair.at[span], pr_send.at[c, g], pr_recv.at[c, g], mate)

        def take(c, g):
            first = along(c, 1, g) * 16
            pair[c, g].wait_recv()

            @pl.loop(0, 4)
            def _(q):
                for u in range(4):
                    k = first + q * 4 + u
                    y_own[c * CHIPS + k] = sums[last_ref[(c * 2 + core) * CHIPS + k]] + r_pair[c * CHIPS + k]

            for w in ways:
                half[c, g, w] = remote(
                    y_own.at[pl.ds(yt(c, g, 2) + 2 * w, 2)],
                    r_ring.at[pl.ds(rt(c, g) + 2 * w, 2)],
                    s3_send.at[c, g, w, 0],
                    s3_recv.at[c, g, w, 0],
                    to(c, 2, w),
                )

        def pass_on(c, g):
            for w in ways:
                half[c, g, w].wait_recv()
                near = yt(c, g, 1 + 2 * w)
                for u in range(2 * w, 2 * w + 2):
                    y_own[near + u] = y_own[near + u] + r_ring[rt(c, g) + u]
                full[c, g, w] = remote(
                    y_own.at[pl.ds(near, 4)],
                    r_ring.at[pl.ds(rt(c, g) + 4 + 4 * w, 4)],
                    s3_send.at[c, g, w, 1],
                    s3_recv.at[c, g, w, 1],
                    to(c, 2, w),
                )

        def settle(c, g):
            for w in ways:
                full[c, g, w].wait_recv()
            here = yt(c, g, 0)
            for u in range(4):
                y_own[here + u] = y_own[here + u] + (r_ring[rt(c, g) + 4 + u] + r_ring[rt(c, g) + 8 + u])

        def take2(c):
            for w in ways:
                half[c, w] = remote(
                    y_own.at[pl.ds(yt(c, 2, 0) + 2 * w, 2)],
                    r_ring.at[pl.ds(rt(c, 4) + 2 * w, 2)],
                    s2_send.at[c, w, 0],
                    s2_recv.at[c, w, 0],
                    to(c, 1, w),
                )

        def pass_on2(c):
            for w in ways:
                half[c, w].wait_recv()
                near = yt(c, 1 + 2 * w, 0)
                for u in range(2 * w, 2 * w + 2):
                    y_own[near + u] = y_own[near + u] + r_ring[rt(c, 4) + u]
                full[c, w] = remote(
                    y_own.at[pl.ds(near, 4)],
                    r_ring.at[pl.ds(rt(c, 4) + 4 + 4 * w, 4)],
                    s2_send.at[c, w, 1],
                    s2_recv.at[c, w, 1],
                    to(c, 1, w),
                )

        def settle2(c):
            for w in ways:
                full[c, w].wait_recv()
            here = yt(c, 0, 0)
            for u in range(4):
                y_own[here + u] = y_own[here + u] + (r_ring[rt(c, 4) + 4 + u] + r_ring[rt(c, 4) + 8 + u])

        for g in GROUPS:
            for c in everyone:
                give(c, g)
        plan = (
            (take, 2),
            (take, 1),
            (pass_on, 2),
            (take, 3),
            (pass_on, 1),
            (take, 0),
            (settle, 2),
            (take2,),
            (pass_on, 3),
            (pass_on, 0),
            (settle, 1),
            (settle, 3),
            (pass_on2,),
            (settle, 0),
            (settle2,),
        )
        for act, *group in plan:
            for c in everyone:
                act(c, *group)
        last = {}
        for c in everyone:
            for step in (1, 3, 2):
                last[c, step] = remote(
                    y_own.at[pl.ds(yt(c, 0, 0) + along(c, 0, step), 1)],
                    r_ring.at[pl.ds(rt(c, 5) + step - 1, 1)],
                    s1_send.at[c, step - 1],
                    s1_recv.at[c, step - 1],
                    at(ORDERS[c][0], step),
                )
        for c in everyone:
            for step in (1, 3, 2):
                last[c, step].wait_recv()
            got = (r_ring[rt(c, 5)] + r_ring[rt(c, 5) + 1]) + r_ring[rt(c, 5) + 2]
            total = y_own[yt(c, 0, 0) + along(c, 0, 0)] + got
            flux = relax_ref[:, lanes(c)] * (driving_ref[:, lanes(c)] + total)
            flux_ref[:, lanes(c)] = flux
            x_all[own[c]] = flux
        drain()

    def sweep_once(sweep, carry):
        gather(sweep)
        multiply()
        scatter()
        return carry

    lax.fori_loop(0, ITERS, sweep_once, 0)

    part, weight = 0.0, 0.0
    for c in everyone:
        part = part + heat_ref[:, lanes(c)] * flux_ref[:, lanes(c)]
        weight = weight + heat_ref[:, lanes(c)]
    stacked = jnp.concatenate([part, jnp.broadcast_to(weight, (TILE - TEMPS, TILE))], axis=0)
    total = lax.dot_general(
        jnp.ones((8, TILE), jnp.float32),
        stacked,
        NT,
        precision=lax.Precision.HIGHEST,
        preferred_element_type=jnp.float32,
    )
    base = 0
    row = [chip_row(k) for k in range(8)]
    for s, (size, here, others) in enumerate(
        (
            (8, coords["x"] * 2 + core, row[1:]),
            (RING, coords["y"], [at("y", k) for k in (1, 2, 3)]),
            (RING, coords["z"], [at("z", k) for k in (1, 2, 3)]),
        )
    ):
        ref = c_all.at[base + here]
        ref[...] = total
        copies = [
            remote(ref, ref, c_send.at[s, k], c_recv.at[s, k], peer) for k, peer in enumerate(others)
        ]
        for copy in copies:
            copy.wait_recv()
        total = c_all[base]
        for k in range(1, size):
            total = total + c_all[base + k]
        base += size
    cond_ref[...] = total
    drain()


def index_of(device, color, strides):
    coords = {"z": device // 32, "y": device // 8 % 4, "x": device // 2 % 4}
    spots = [place(coords, c, strides) for c in range(COLORS)]
    spot = jnp.where(color == 0, spots[0], jnp.where(color == 1, spots[1], spots[2]))
    return (color * 2 + device % 2) * CHIPS + spot


def shards(tile_values, tile_owner, tile_row, tile_col, tile_count, relaxation, driving, heat_weight):
    owner = tile_owner[:, 0]
    slots = jnp.arange(SLOTS, dtype=jnp.int32)
    is_used = slots < tile_count[0]
    row = (owner // 8) * ROWT_DEV + tile_row
    key = jnp.where(is_used, index_of(row // COLORS, row % COLORS, Y_STRIDES), 2 * HALF)
    xs = index_of((tile_col // COLORS) * 8 + owner % 8, tile_col % COLORS, X_STRIDES)
    before = (key[None, :] < key[:, None]) | ((key[None, :] == key[:, None]) & (slots[None, :] < slots[:, None]))
    rank = jnp.sum(before.astype(jnp.int32), axis=1)
    is_here = (rank[None, :] == slots[:, None]).astype(jnp.int32)
    order = jnp.sum(is_here * slots[None, :], axis=1)
    xs = jnp.sum(is_here * xs[None, :], axis=1)
    keys = jnp.sum(is_here * key[None, :], axis=1)
    first = (keys != jnp.concatenate([jnp.full((1,), -1, jnp.int32), keys[:-1]])).astype(jnp.int32)
    rows = jnp.arange(2 * HALF, dtype=jnp.int32)
    upto = jnp.sum((key[None, :] <= rows[:, None]).astype(jnp.int32), axis=1)
    has = jnp.any(key[None, :] == rows[:, None], axis=1)
    last = jnp.where(has, upto - 1, SLOTS)

    smem = pl.BlockSpec(memory_space=pltpu.SMEM)
    vmem = pl.BlockSpec(memory_space=pltpu.VMEM)
    f32 = jnp.float32
    dma = pltpu.SemaphoreType.DMA
    flux, cond = pl.pallas_call(
        kernel,
        out_shape=(
            jax.ShapeDtypeStruct((TEMPS, COLORS * TILE), f32),
            jax.ShapeDtypeStruct((8, TILE), f32),
        ),
        in_specs=[smem] * 4 + [pl.BlockSpec(memory_space=pl.ANY)] + [vmem] * 3,
        out_specs=(vmem, vmem),
        scratch_shapes=[
            pltpu.VMEM((SLOTS, TILE, TILE), f32),
            pltpu.VMEM((SLOTS, TILE, TILE), jnp.bfloat16),
            pltpu.VMEM((SLOTS, TILE, TILE), jnp.bfloat16),
            pltpu.VMEM((2 * HALF, TEMPS, TILE), f32),
            pltpu.VMEM((SLOTS + 1, TEMPS, TILE), f32),
            pltpu.VMEM((HALF, TEMPS, TILE), f32),
            pltpu.VMEM((HALF, TEMPS, TILE), f32),
            pltpu.VMEM((HALF, TEMPS, TILE), f32),
            pltpu.VMEM((COLORS * RING_TILES, TEMPS, TILE), f32),
            pltpu.VMEM((16, 8, TILE), f32),
            dma,
            dma((COLORS, 3)),
            dma((COLORS, 3)),
            dma((COLORS, 2, 2)),
            dma((COLORS, 2, 2)),
            dma((COLORS, 4, 2, 2)),
            dma((COLORS, 4, 2, 2)),
            dma((COLORS, 13)),
            dma((COLORS, 13)),
            dma((COLORS, 4)),
            dma((COLORS, 4)),
            dma((COLORS, 4, 2, 2)),
            dma((COLORS, 4, 2, 2)),
            dma((COLORS, 2, 2)),
            dma((COLORS, 2, 2)),
            dma((COLORS, 3)),
            dma((COLORS, 3)),
            dma((3, 7)),
            dma((3, 7)),
        ],
        compiler_params=pltpu.CompilerParams(
            collective_id=0, has_side_effects=True, vmem_limit_bytes=67043328
        ),
        name="solve",
    )(
        order,
        xs,
        first,
        last,
        tile_values,
        driving.T,
        relaxation.reshape(1, COLORS * TILE),
        heat_weight.reshape(1, COLORS * TILE),
    )
    return flux.T, cond[0, :TEMPS] / cond[0, TEMPS]


def solution(mesh):
    torus = Mesh(mesh.devices.reshape(4, 4, 4, 2), AXES)
    placed = (
        P(AXES, None, None),
        P(AXES, None),
        P(AXES),
        P(AXES),
        P(AXES),
        P(AXES),
        P(AXES, None),
        P(AXES),
    )
    return jax.shard_map(
        shards, mesh=torus, in_specs=placed, out_specs=(P(AXES, None), P()), check_vma=False
    )
```

time: 308 us -> 240 us (0.78)
  Pallas kernels: 296 us -> 228 us
    pallas_call x1, Pallas kernels: 296 us -> 228 us  [shards(): pl.pallas_call(kernel, out_shape=(jax.ShapeDtypeStruct((TEMPS, COLORS * T...]
where the time goes in v2:
time: 240 us; the launch traced here: 239 us
  Pallas kernels  228 us (95%)
  local copies, waits for them, and re-layouts  5.35 us (2%)
  other arithmetic  5.02 us (2%)
    pallas_call x1, Pallas kernels, shards(): pl.pallas_call(kernel, out_shape=(jax.ShapeDtypeStruct((TEMPS, COLORS * T...  228 us

profile of v2, /device:TPU:0, one launch (start us, length us, event | category | flops | bytes accessed | tf_op | source)
XLA Modules:
  0.0 239.2 jit_solution(5217312960088937501)
XLA Ops:
  1.3 0.7 fusion.7
  2.0 0.2 convert_reduce_fusion.1
  2.2 0.7 select_reduce_fusion
  2.9 0.6 compare_convert_fusion.first_ref
  3.6 0.1 convert_reduce_fusion
  3.7 0.2 fusion
  3.9 0.6 add_select_fusion.last_ref
  4.5 1.3 reshape.16.relax_ref
  5.7 1.3 reshape.17.heat_ref
  7.0 227.6 %solve.1 = (f32[64,384]{1,0:T(8,128)}, f32[8,128]{1,0:T(8,128)}) custom-call(s32[128]{0:T(128)} %get-tuple-element.8.order_ref, s32[128]{0:T(128)} %get-tuple-element.7.xs_ref, s32[128]{0:T(128)} %compare_convert_fusion.first_ref, s32[384]{0:T(512)} %add_select_fusion.last_ref, f32[128,128,128]{2,1,0:T(8,128)} %tiles_hbm.1, f32[64,384]{1,0:T(8,128)} %bitcast.25, ...), custom_call_target="tpu_custom_call" | custom-call | tf_op jit(solution)/shard_map/solve/pallas_call | solution.py:443
  234.6 1.3 slice.11
  235.8 1.8 divide_bitcast_fusion
  237.7 1.5 copy.12

commit v3 on v2

--- a/solution.py
+++ b/solution.py
@@ -20,6 +20,9 @@
 GROUPS = (2, 1, 3, 0)
 RING_TILES = 63
 NT = (((1,), (1,)), ((), ()))
+NN = (((1,), (0,)), ((), ()))
+STEPS = (1, 3, 2)
+PARTS = 4
 MESH = pl.DeviceIdType.MESH
 
 
@@ -36,6 +39,7 @@
     order_ref,
     xs_ref,
     first_ref,
+    hr_index_ref,
     last_ref,
     tiles_hbm,
     driving_ref,
@@ -44,14 +48,15 @@
     flux_ref,
     cond_ref,
     stage,
-    t_hi,
-    t_lo,
+    t_both,
     x_all,
     sums,
     y_own,
     y_pair,
     r_pair,
     r_ring,
+    hr_all,
+    part_ref,
     c_all,
     stage_sem,
     g1_send,
@@ -70,6 +75,8 @@
     s2_recv,
     s1_send,
     s1_recv,
+    h_send,
+    h_recv,
     c_send,
     c_recv,
 ):
@@ -95,10 +102,21 @@
     def lanes(c):
         return slice(c * TILE, (c + 1) * TILE)
 
+    def relax(c):
+        return relax_ref[lanes(c)].reshape(1, TILE)
+
+    def heat(c):
+        return heat_ref[lanes(c)].reshape(1, TILE)
+
+    h_base = core * HALF
+    h_own = h_base + place(coords, 0, X_STRIDES) * COLORS
+
     own = [(c * 2 + core) * CHIPS + place(coords, c, X_STRIDES) for c in range(COLORS)]
     for c in range(COLORS):
-        x_all[own[c]] = relax_ref[:, lanes(c)] * driving_ref[:, lanes(c)]
+        x_all[own[c]] = relax(c) * driving_ref[:, lanes(c)]
+        hr_all[h_own + c] = heat(c) * relax(c)
     sums[SLOTS] = jnp.zeros((TEMPS, TILE), jnp.float32)
+    hr_all[2 * HALF] = jnp.zeros((1, TILE), jnp.float32)
     pl.semaphore_wait(barrier, len(peers))
 
     def along(c, p, step):
@@ -106,10 +124,13 @@
 
     sends = []
 
-    def remote(src, dst, ssem, rsem, device):
-        copy = pltpu.make_async_remote_copy(
+    def plain(src, dst, ssem, rsem, device):
+        return pltpu.make_async_remote_copy(
             src_ref=src, dst_ref=dst, send_sem=ssem, recv_sem=rsem, device_id=device, device_id_type=MESH
         )
+
+    def remote(*args):
+        copy = plain(*args)
         copy.start()
         sends.append(copy)
         return copy
@@ -122,15 +143,45 @@
     def to(c, p, way):
         return at(ORDERS[c][p], 1 + 2 * way)
 
-    def split_tiles():
-        load.wait()
-
-        @pl.loop(0, SLOTS)
+    def split_tiles(part):
+        if part == 0:
+            load.wait()
+
+        @pl.loop(part * SLOTS // PARTS, (part + 1) * SLOTS // PARTS)
         def _(j):
-            tile = stage[order_ref[j]]
+            tile = stage[order_ref[j]].T
             hi = tile.astype(jnp.bfloat16)
-            t_hi[j] = hi
-            t_lo[j] = (tile - hi.astype(jnp.float32)).astype(jnp.bfloat16)
+            t_both[j, :TILE] = hi
+            t_both[j, TILE:] = (tile - hi.astype(jnp.float32)).astype(jnp.bfloat16)
+
+    def weights(stage_of):
+        axis = ("x", "y", "z")[stage_of]
+        first = h_base + COLORS * (
+            coords["x"] * (stage_of < 1) + coords["y"] * 4 * (stage_of < 2) + coords["z"] * 16
+        )
+        ref = hr_all.at[pl.ds(first, COLORS * 4**stage_of)]
+        return [
+            plain(ref, ref, h_send.at[stage_of, step - 1], h_recv.at[stage_of, step - 1], at(axis, step))
+            for step in STEPS
+        ]
+
+    def weights_to_mate():
+        ref = hr_all.at[pl.ds(h_base, HALF)]
+        return [plain(ref, ref, h_send.at[3, 0], h_recv.at[3, 0], mate)]
+
+    def start(copies):
+        for copy in copies:
+            copy.start()
+
+    def receive(copies):
+        for copy in copies:
+            copy.wait_recv()
+
+    def first_only(sweep, *acts):
+        @pl.when(sweep == 0)
+        def _():
+            for act in acts:
+                act()
 
     everyone = range(COLORS)
     ways = (0, 1)
@@ -181,6 +232,7 @@
                 far[c, w] = remote(ref, ref, g2_send.at[c, w, 0], g2_recv.at[c, w, 0], to(c, 1, w))
         for c in everyone:
             block(c, 0)
+        first_only(sweep, lambda: receive(weights(0)), lambda: start(weights(1)), lambda: split_tiles(0))
         for c in everyone:
             for w in ways:
                 far[c, w].wait_recv()
@@ -189,7 +241,7 @@
         for g in (3, 1):
             for c in everyone:
                 block(c, g)
-        pl.when(sweep == 0)(split_tiles)
+        first_only(sweep, lambda: receive(weights(1)), lambda: start(weights(2)), lambda: split_tiles(1))
         for c in everyone:
             relay(c, 0)
         for c in everyone:
@@ -197,6 +249,7 @@
                 far[c, w].wait_recv()
             block(c, 2)
             forward(c, 0, (c * 2 + core) * CHIPS + along(c, 2, 0) * 16, 16)
+        first_only(sweep, lambda: receive(weights(2)), lambda: start(weights_to_mate()), lambda: split_tiles(2))
         for g in (3, 1):
             for c in everyone:
                 relay(c, g)
@@ -204,9 +257,11 @@
             arrived(c, 0)
         for c in everyone:
             relay(c, 2)
+        first_only(sweep, lambda: split_tiles(3))
         for g in (3, 1, 2):
             for c in everyone:
                 arrived(c, g)
+        first_only(sweep, lambda: receive(weights_to_mate()))
         for copy in forwards:
             copy.wait_recv()
         drain()
@@ -214,24 +269,69 @@
     def multiply():
         unroll = 8
 
-        def some(g, acc):
+        def some(g, carry):
+            acc, part = carry
             for u in range(unroll):
                 j = g * unroll + u
                 x = x_all[xs_ref[j]]
                 hi = x.astype(jnp.bfloat16)
                 lo = (x - hi.astype(jnp.float32)).astype(jnp.bfloat16)
-                both = lax.dot_general(
-                    jnp.concatenate([hi, lo], axis=0), t_hi[j], NT, preferred_element_type=jnp.float32
-                )
-                rest = lax.dot_general(hi, t_lo[j], NT, preferred_element_type=jnp.float32)
-                prod = both[:TEMPS] + both[TEMPS:] + rest
+                prod = lax.dot_general(
+                    jnp.concatenate([hi, hi], axis=1), t_both[j], NN, preferred_element_type=jnp.float32
+                ) + lax.dot_general(lo, t_both[j, :TILE], NN, preferred_element_type=jnp.float32)
                 acc = jnp.where(first_ref[j] != 0, 0.0, acc) + prod
+                part = part + prod * hr_all[hr_index_ref[j]]
                 sums[j] = acc
-            return acc
-
-        lax.fori_loop(0, SLOTS // unroll, some, jnp.zeros((TEMPS, TILE), jnp.float32))
-
-    def scatter():
+            return acc, part
+
+        zero = jnp.zeros((TEMPS, TILE), jnp.float32)
+        part_ref[...] = lax.fori_loop(0, SLOTS // unroll, some, (zero, zero))[1]
+
+    row = [chip_row(k) for k in range(8)]
+    rounds = (
+        (0, 8, coords["x"] * 2 + core, row[1:]),
+        (8, RING, coords["y"], [at("y", k) for k in (1, 2, 3)]),
+        (12, RING, coords["z"], [at("z", k) for k in (1, 2, 3)]),
+    )
+
+    def totals(k):
+        base, _, here, others = rounds[k]
+        ref = c_all.at[base + here]
+        return [plain(ref, ref, c_send.at[k, i], c_recv.at[k, i], peer) for i, peer in enumerate(others)]
+
+    def first_total():
+        part, weight = part_ref[...], 0.0
+        for c in range(COLORS):
+            part = part + heat(c) * relax(c) * driving_ref[:, lanes(c)]
+            weight = weight + heat(c)
+        ones = jnp.ones((8, TILE), jnp.float32)
+
+        def lane_sum(rows):
+            return lax.dot_general(
+                ones, rows, NT, precision=lax.Precision.HIGHEST, preferred_element_type=jnp.float32
+            )
+
+        over = lane_sum(jnp.concatenate([part, part], axis=0))
+        under = lane_sum(jnp.broadcast_to(weight, (TILE, TILE)))
+        upper = lax.broadcasted_iota(jnp.int32, (8, TILE), 0) < 4
+        return jnp.where(upper, over, under)
+
+    def round_total(k):
+        base, size = rounds[k][:2]
+        receive(totals(k))
+        total = c_all[base]
+        for i in range(1, size):
+            total = total + c_all[base + i]
+        return total
+
+    def start_round(k):
+        c_all[rounds[k][0] + rounds[k][2]] = first_total() if k == 0 else round_total(k - 1)
+        start(totals(k))
+
+    def last_only(sweep, act):
+        pl.when(sweep == ITERS - 1)(act)
+
+    def scatter(sweep):
         pair, half, full = {}, {}, {}
 
         def yt(c, g, j):
@@ -343,9 +443,11 @@
             (settle, 0),
             (settle2,),
         )
-        for act, *group in plan:
+        for k, (act, *group) in enumerate(plan):
             for c in everyone:
                 act(c, *group)
+            if k in (1, 4, 8):
+                last_only(sweep, lambda k=k: start_round((1, 4, 8).index(k)))
         last = {}
         for c in everyone:
             for step in (1, 3, 2):
@@ -361,7 +463,7 @@
                 last[c, step].wait_recv()
             got = (r_ring[rt(c, 5)] + r_ring[rt(c, 5) + 1]) + r_ring[rt(c, 5) + 2]
             total = y_own[yt(c, 0, 0) + along(c, 0, 0)] + got
-            flux = relax_ref[:, lanes(c)] * (driving_ref[:, lanes(c)] + total)
+            flux = relax(c) * (driving_ref[:, lanes(c)] + total)
             flux_ref[:, lanes(c)] = flux
             x_all[own[c]] = flux
         drain()
@@ -369,45 +471,18 @@
     def sweep_once(sweep, carry):
         gather(sweep)
         multiply()
-        scatter()
+        scatter(sweep)
         return carry
 
+    start(weights(0))
     lax.fori_loop(0, ITERS, sweep_once, 0)
 
-    part, weight = 0.0, 0.0
-    for c in everyone:
-        part = part + heat_ref[:, lanes(c)] * flux_ref[:, lanes(c)]
-        weight = weight + heat_ref[:, lanes(c)]
-    stacked = jnp.concatenate([part, jnp.broadcast_to(weight, (TILE - TEMPS, TILE))], axis=0)
-    total = lax.dot_general(
-        jnp.ones((8, TILE), jnp.float32),
-        stacked,
-        NT,
-        precision=lax.Precision.HIGHEST,
-        preferred_element_type=jnp.float32,
-    )
-    base = 0
-    row = [chip_row(k) for k in range(8)]
-    for s, (size, here, others) in enumerate(
-        (
-            (8, coords["x"] * 2 + core, row[1:]),
-            (RING, coords["y"], [at("y", k) for k in (1, 2, 3)]),
-            (RING, coords["z"], [at("z", k) for k in (1, 2, 3)]),
-        )
-    ):
-        ref = c_all.at[base + here]
-        ref[...] = total
-        copies = [
-            remote(ref, ref, c_send.at[s, k], c_recv.at[s, k], peer) for k, peer in enumerate(others)
-        ]
-        for copy in copies:
-            copy.wait_recv()
-        total = c_all[base]
-        for k in range(1, size):
-            total = total + c_all[base + k]
-        base += size
-    cond_ref[...] = total
-    drain()
+    total = round_total(2)
+    cond_ref[...] = total[0:1] / total[4:5]
+    for k in range(3):
+        for copy in totals(k) + weights(k):
+            copy.wait_send()
+    weights_to_mate()[0].wait_send()
 
 
 def index_of(device, color, strides):
@@ -430,6 +505,10 @@
     order = jnp.sum(is_here * slots[None, :], axis=1)
     xs = jnp.sum(is_here * xs[None, :], axis=1)
     keys = jnp.sum(is_here * key[None, :], axis=1)
+    device, color = row // COLORS, row % COLORS
+    spot = {"z": device // 32, "y": device // 8 % 4, "x": device // 2 % 4}
+    hr_index = (device % 2 * CHIPS + place(spot, 0, X_STRIDES)) * COLORS + color
+    hr_index = jnp.sum(is_here * jnp.where(is_used, hr_index, 2 * HALF)[None, :], axis=1)
     first = (keys != jnp.concatenate([jnp.full((1,), -1, jnp.int32), keys[:-1]])).astype(jnp.int32)
     rows = jnp.arange(2 * HALF, dtype=jnp.int32)
     upto = jnp.sum((key[None, :] <= rows[:, None]).astype(jnp.int32), axis=1)
@@ -444,20 +523,21 @@
         kernel,
         out_shape=(
             jax.ShapeDtypeStruct((TEMPS, COLORS * TILE), f32),
-            jax.ShapeDtypeStruct((8, TILE), f32),
+            jax.ShapeDtypeStruct((1, TILE), f32),
         ),
-        in_specs=[smem] * 4 + [pl.BlockSpec(memory_space=pl.ANY)] + [vmem] * 3,
+        in_specs=[smem] * 5 + [pl.BlockSpec(memory_space=pl.ANY)] + [vmem] * 3,
         out_specs=(vmem, vmem),
         scratch_shapes=[
             pltpu.VMEM((SLOTS, TILE, TILE), f32),
-            pltpu.VMEM((SLOTS, TILE, TILE), jnp.bfloat16),
-            pltpu.VMEM((SLOTS, TILE, TILE), jnp.bfloat16),
+            pltpu.VMEM((SLOTS, 2 * TILE, TILE), jnp.bfloat16),
             pltpu.VMEM((2 * HALF, TEMPS, TILE), f32),
             pltpu.VMEM((SLOTS + 1, TEMPS, TILE), f32),
             pltpu.VMEM((HALF, TEMPS, TILE), f32),
             pltpu.VMEM((HALF, TEMPS, TILE), f32),
             pltpu.VMEM((HALF, TEMPS, TILE), f32),
             pltpu.VMEM((COLORS * RING_TILES, TEMPS, TILE), f32),
+            pltpu.VMEM((2 * HALF + 1, 1, TILE), f32),
+            pltpu.VMEM((TEMPS, TILE), f32),
             pltpu.VMEM((16, 8, TILE), f32),
             dma,
             dma((COLORS, 3)),
@@ -476,6 +556,8 @@
             dma((COLORS, 2, 2)),
             dma((COLORS, 3)),
             dma((COLORS, 3)),
+            dma((4, 3)),
+            dma((4, 3)),
             dma((3, 7)),
             dma((3, 7)),
         ],
@@ -487,13 +569,14 @@
         order,
         xs,
         first,
+        hr_index,
         last,
         tile_values,
         driving.T,
-        relaxation.reshape(1, COLORS * TILE),
-        heat_weight.reshape(1, COLORS * TILE),
+        relaxation,
+        heat_weight,
     )
-    return flux.T, cond[0, :TEMPS] / cond[0, TEMPS]
+    return flux.T, cond[0, :TEMPS]
 
 
 def solution(mesh):

time: 240 us -> 219 us (0.912)
  Pallas kernels: 228 us -> 211 us
  local copies, waits for them, and re-layouts: 5.35 us -> 2.72 us
    pallas_call x1, Pallas kernels: 228 us -> 211 us  [shards(): pl.pallas_call(kernel, out_shape=(jax.ShapeDtypeStruct((TEMPS, COLORS * T...]
    reshape x2 -> x0, local copies, waits for them, and re-layouts: 2.54 us -> none  [the longest x1 1.27 us: shards(): relaxation.reshape(1, COLORS * TILE)]
where the time goes in v3:
time: 219 us
  Pallas kernels  211 us (96%)
  other arithmetic  3.15 us (1%)
  local copies, waits for them, and re-layouts  2.72 us (1%)
    pallas_call x1, Pallas kernels, shards(): pl.pallas_call(kernel, out_shape=(jax.ShapeDtypeStruct((TEMPS, COLORS * T...  211 us

profile of v3, /device:TPU:0, one launch (start us, length us, event | category | flops | bytes accessed | tf_op | source)
XLA Modules:
  0.0 218.6 jit_solution(4184628392733615789)
XLA Ops:
  1.3 0.7 compare_select_fusion.16
  2.0 0.1 fusion
  2.2 0.2 convert_reduce_fusion.1
  2.4 0.8 select_reduce_fusion
  3.1 0.6 compare_convert_fusion.first_ref
  3.7 0.1 convert_reduce_fusion
  3.9 0.6 add_select_fusion.last_ref
  4.4 211.5 %solve.1 = (f32[64,384]{1,0:T(8,128)}, f32[1,128]{1,0:T(1,128)}) custom-call(s32[128]{0:T(128)} %get-tuple-element.9.order_ref, s32[128]{0:T(128)} %get-tuple-element.8.xs_ref, s32[128]{0:T(128)} %compare_convert_fusion.first_ref, s32[128]{0:T(128)} %get-tuple-element.6.hr_index_ref, s32[384]{0:T(512)} %add_select_fusion.last_ref, ...), custom_call_target="tpu_custom_call" | custom-call | tf_op jit(solution)/shard_map/solve/pallas_call | solution.py:522
  215.9 1.2 slice_bitcast_fusion
  217.1 1.5 copy.12
  (1 shorter events, 0.0 us)

commit v4 on v3

--- a/solution.py
+++ b/solution.py
@@ -340,31 +340,27 @@
         def rt(c, g):
             return c * RING_TILES + g * 12
 
-        def give(c, g):
-            first = along(c, 1, g) * 16
-
-            @pl.loop(0, 4)
-            def _(q):
-                for u in range(4):
-                    k = first + q * 4 + u
-                    y_pair[c * CHIPS + k] = sums[last_ref[(c * 2 + 1 - core) * CHIPS + k]]
-
-            span = pl.ds(c * CHIPS + first, 16)
-            pair[c, g] = remote(y_pair.at[span], r_pair.at[span], pr_send.at[c, g], pr_recv.at[c, g], mate)
+        def give(c, g, j):
+            first = yt(c, g, j)
+            for u in range(4):
+                y_pair[first + u] = sums[last_ref[c * CHIPS + (1 - core) * CHIPS + first + u]]
+            span = pl.ds(first, 4)
+            pair[c, g, j] = remote(y_pair.at[span], r_pair.at[span], pr_send.at[c, g, j], pr_recv.at[c, g, j], mate)
+
+        def both_cores(c, g, j):
+            first = yt(c, g, j)
+            pair[c, g, j].wait_recv()
+            return first, [
+                sums[last_ref[c * CHIPS + core * CHIPS + first + u]] + r_pair[first + u] for u in range(4)
+            ]
 
         def take(c, g):
-            first = along(c, 1, g) * 16
-            pair[c, g].wait_recv()
-
-            @pl.loop(0, 4)
-            def _(q):
-                for u in range(4):
-                    k = first + q * 4 + u
-                    y_own[c * CHIPS + k] = sums[last_ref[(c * 2 + core) * CHIPS + k]] + r_pair[c * CHIPS + k]
-
+            first, rows = both_cores(c, g, 2)
+            for u in range(4):
+                y_own[first + u] = rows[u]
             for w in ways:
                 half[c, g, w] = remote(
-                    y_own.at[pl.ds(yt(c, g, 2) + 2 * w, 2)],
+                    y_own.at[pl.ds(first + 2 * w, 2)],
                     r_ring.at[pl.ds(rt(c, g) + 2 * w, 2)],
                     s3_send.at[c, g, w, 0],
                     s3_recv.at[c, g, w, 0],
@@ -373,10 +369,10 @@
 
         def pass_on(c, g):
             for w in ways:
+                near, rows = both_cores(c, g, 1 + 2 * w)
                 half[c, g, w].wait_recv()
-                near = yt(c, g, 1 + 2 * w)
-                for u in range(2 * w, 2 * w + 2):
-                    y_own[near + u] = y_own[near + u] + r_ring[rt(c, g) + u]
+                for u in range(4):
+                    y_own[near + u] = rows[u] + r_ring[rt(c, g) + u] if u // 2 == w else rows[u]
                 full[c, g, w] = remote(
                     y_own.at[pl.ds(near, 4)],
                     r_ring.at[pl.ds(rt(c, g) + 4 + 4 * w, 4)],
@@ -386,11 +382,11 @@
                 )
 
         def settle(c, g):
+            here, rows = both_cores(c, g, 0)
             for w in ways:
                 full[c, g, w].wait_recv()
-            here = yt(c, g, 0)
             for u in range(4):
-                y_own[here + u] = y_own[here + u] + (r_ring[rt(c, g) + 4 + u] + r_ring[rt(c, g) + 8 + u])
+                y_own[here + u] = rows[u] + (r_ring[rt(c, g) + 4 + u] + r_ring[rt(c, g) + 8 + u])
 
         def take2(c):
             for w in ways:
@@ -423,19 +419,24 @@
             for u in range(4):
                 y_own[here + u] = y_own[here + u] + (r_ring[rt(c, 4) + 4 + u] + r_ring[rt(c, 4) + 8 + u])
 
-        for g in GROUPS:
-            for c in everyone:
-                give(c, g)
+        for j, groups in ((2, GROUPS), (1, (2,)), (3, (2,)), (1, (1,)), (3, (1,)), (1, (3,)), (3, (3,))):
+            for g in groups:
+                for c in everyone:
+                    give(c, g, j)
+        for j, groups in ((0, (2,)), (1, (0,)), (3, (0,)), (0, (1, 3, 0))):
+            for g in groups:
+                for c in everyone:
+                    give(c, g, j)
         plan = (
             (take, 2),
             (take, 1),
+            (take, 3),
+            (take, 0),
             (pass_on, 2),
-            (take, 3),
             (pass_on, 1),
-            (take, 0),
+            (pass_on, 3),
             (settle, 2),
             (take2,),
-            (pass_on, 3),
             (pass_on, 0),
             (settle, 1),
             (settle, 3),
@@ -446,8 +447,8 @@
         for k, (act, *group) in enumerate(plan):
             for c in everyone:
                 act(c, *group)
-            if k in (1, 4, 8):
-                last_only(sweep, lambda k=k: start_round((1, 4, 8).index(k)))
+            if k in (3, 7, 10):
+                last_only(sweep, lambda k=k: start_round((3, 7, 10).index(k)))
         last = {}
         for c in everyone:
             for step in (1, 3, 2):
@@ -548,8 +549,8 @@
             dma((COLORS, 4, 2, 2)),
             dma((COLORS, 13)),
             dma((COLORS, 13)),
-            dma((COLORS, 4)),
-            dma((COLORS, 4)),
+            dma((COLORS, 4, 4)),
+            dma((COLORS, 4, 4)),
             dma((COLORS, 4, 2, 2)),
             dma((COLORS, 4, 2, 2)),
             dma((COLORS, 2, 2)),

time: 219 us -> 211 us (0.963)
  Pallas kernels: 211 us -> 204 us
    pallas_call x1, Pallas kernels: 211 us -> 204 us  [shards(): pl.pallas_call(kernel, out_shape=(jax.ShapeDtypeStruct((TEMPS, COLORS * T...]
where the time goes in v4:
time: 211 us
  Pallas kernels  204 us (97%)
  other arithmetic  3.15 us (1%)
  local copies, waits for them, and re-layouts  2.72 us (1%)
    pallas_call x1, Pallas kernels, shards(): pl.pallas_call(kernel, out_shape=(jax.ShapeDtypeStruct((TEMPS, COLORS * T...  204 us

profile of v4, /device:TPU:0, one launch (start us, length us, event | category | flops | bytes accessed | tf_op | source)
XLA Modules:
  0.0 211.2 jit_solution(3013568738606114704)
XLA Ops:
  1.3 0.7 compare_select_fusion.16
  2.0 0.1 fusion
  2.2 0.2 convert_reduce_fusion.1
  2.4 0.8 select_reduce_fusion
  3.1 0.6 compare_convert_fusion.first_ref
  3.7 0.1 convert_reduce_fusion
  3.9 0.6 add_select_fusion.last_ref
  4.4 204.0 %solve.1 = (f32[64,384]{1,0:T(8,128)}, f32[1,128]{1,0:T(1,128)}) custom-call(s32[128]{0:T(128)} %get-tuple-element.9.order_ref, s32[128]{0:T(128)} %get-tuple-element.8.xs_ref, s32[128]{0:T(128)} %compare_convert_fusion.first_ref, s32[128]{0:T(128)} %get-tuple-element.6.hr_index_ref, s32[384]{0:T(512)} %add_select_fusion.last_ref, ...), custom_call_target="tpu_custom_call" | custom-call | tf_op jit(solution)/shard_map/solve/pallas_call | solution.py:523
  208.4 1.2 slice_bitcast_fusion
  209.6 1.5 copy.12
  (1 shorter events, 0.0 us)

commit v5 on v4

--- a/solution.py
+++ b/solution.py
@@ -38,7 +38,7 @@
 def kernel(
     order_ref,
     xs_ref,
-    first_ref,
+    keys_ref,
     hr_index_ref,
     last_ref,
     tiles_hbm,
@@ -224,20 +224,26 @@
                 near[c, step] = remote(
                     ref, ref, g1_send.at[c, step - 1], g1_recv.at[c, step - 1], at(ORDERS[c][0], step)
                 )
-        for c in everyone:
-            for step in (1, 3, 2):
+        def send2(c, i, k):
+            ref = tiles(xt(c, 0, 0) + along(c, 0, k), 1)
+            for w in ways:
+                far[c, w, i] = remote(ref, ref, g2_send.at[c, w, 1 + i], g2_recv.at[c, w, 1 + i], to(c, 1, w))
+
+        for c in everyone:
+            send2(c, 0, 0)
+        for step in (1, 3, 2):
+            for c in everyone:
                 near[c, step].wait_recv()
-            for w in ways:
-                ref = tiles(xt(c, 0, 0), 4)
-                far[c, w] = remote(ref, ref, g2_send.at[c, w, 0], g2_recv.at[c, w, 0], to(c, 1, w))
+                send2(c, step, 4 - step)
         for c in everyone:
             block(c, 0)
         first_only(sweep, lambda: receive(weights(0)), lambda: start(weights(1)), lambda: split_tiles(0))
         for c in everyone:
             for w in ways:
-                far[c, w].wait_recv()
+                for i in range(4):
+                    far[c, w, i].wait_recv()
                 ref = tiles(xt(c, 0, 3 - 2 * w) + 2 * w, 2)
-                far[c, w] = remote(ref, ref, g2_send.at[c, w, 1], g2_recv.at[c, w, 1], to(c, 1, w))
+                far[c, w] = remote(ref, ref, g2_send.at[c, w, 0], g2_recv.at[c, w, 0], to(c, 1, w))
         for g in (3, 1):
             for c in everyone:
                 block(c, g)
@@ -267,7 +273,7 @@
         drain()
 
     def multiply():
-        unroll = 8
+        unroll = 32
 
         def some(g, carry):
             acc, part = carry
@@ -279,7 +285,7 @@
                 prod = lax.dot_general(
                     jnp.concatenate([hi, hi], axis=1), t_both[j], NN, preferred_element_type=jnp.float32
                 ) + lax.dot_general(lo, t_both[j, :TILE], NN, preferred_element_type=jnp.float32)
-                acc = jnp.where(first_ref[j] != 0, 0.0, acc) + prod
+                acc = jnp.where(keys_ref[j] != keys_ref[lax.max(j - 1, 0)], 0.0, acc) + prod
                 part = part + prod * hr_all[hr_index_ref[j]]
                 sums[j] = acc
             return acc, part
@@ -332,7 +338,7 @@
         pl.when(sweep == ITERS - 1)(act)
 
     def scatter(sweep):
-        pair, half, full = {}, {}, {}
+        pair, half, full, tail, last = {}, {}, {}, {}, {}
 
         def yt(c, g, j):
             return c * CHIPS + along(c, 1, g) * 16 + along(c, 2, j) * 4
@@ -404,20 +410,31 @@
                 near = yt(c, 1 + 2 * w, 0)
                 for u in range(2 * w, 2 * w + 2):
                     y_own[near + u] = y_own[near + u] + r_ring[rt(c, 4) + u]
-                full[c, w] = remote(
-                    y_own.at[pl.ds(near, 4)],
-                    r_ring.at[pl.ds(rt(c, 4) + 4 + 4 * w, 4)],
-                    s2_send.at[c, w, 1],
-                    s2_recv.at[c, w, 1],
-                    to(c, 1, w),
+            for step in (2, 1, 3, 0):
+                for w in ways:
+                    k = along(c, 0, step)
+                    tail[c, w, step] = remote(
+                        y_own.at[pl.ds(yt(c, 1 + 2 * w, 0) + k, 1)],
+                        r_ring.at[pl.ds(rt(c, 4) + 4 + 4 * w + k, 1)],
+                        s2_send.at[c, w, 1 + step],
+                        s2_recv.at[c, w, 1 + step],
+                        to(c, 1, w),
+                    )
+
+        def settle2(c, step):
+            for w in ways:
+                tail[c, w, step].wait_recv()
+            k = along(c, 0, step)
+            here = yt(c, 0, 0) + k
+            y_own[here] = y_own[here] + (r_ring[rt(c, 4) + 4 + k] + r_ring[rt(c, 4) + 8 + k])
+            if step:
+                last[c, step] = remote(
+                    y_own.at[pl.ds(here, 1)],
+                    r_ring.at[pl.ds(rt(c, 5) + step - 1, 1)],
+                    s1_send.at[c, step - 1],
+                    s1_recv.at[c, step - 1],
+                    at(ORDERS[c][0], step),
                 )
-
-        def settle2(c):
-            for w in ways:
-                full[c, w].wait_recv()
-            here = yt(c, 0, 0)
-            for u in range(4):
-                y_own[here + u] = y_own[here + u] + (r_ring[rt(c, 4) + 4 + u] + r_ring[rt(c, 4) + 8 + u])
 
         for j, groups in ((2, GROUPS), (1, (2,)), (3, (2,)), (1, (1,)), (3, (1,)), (1, (3,)), (3, (3,))):
             for g in groups:
@@ -442,23 +459,16 @@
             (settle, 3),
             (pass_on2,),
             (settle, 0),
-            (settle2,),
+            (settle2, 2),
+            (settle2, 1),
+            (settle2, 3),
+            (settle2, 0),
         )
         for k, (act, *group) in enumerate(plan):
             for c in everyone:
                 act(c, *group)
             if k in (3, 7, 10):
                 last_only(sweep, lambda k=k: start_round((3, 7, 10).index(k)))
-        last = {}
-        for c in everyone:
-            for step in (1, 3, 2):
-                last[c, step] = remote(
-                    y_own.at[pl.ds(yt(c, 0, 0) + along(c, 0, step), 1)],
-                    r_ring.at[pl.ds(rt(c, 5) + step - 1, 1)],
-                    s1_send.at[c, step - 1],
-                    s1_recv.at[c, step - 1],
-                    at(ORDERS[c][0], step),
-                )
         for c in everyone:
             for step in (1, 3, 2):
                 last[c, step].wait_recv()
@@ -510,7 +520,6 @@
     spot = {"z": device // 32, "y": device // 8 % 4, "x": device // 2 % 4}
     hr_index = (device % 2 * CHIPS + place(spot, 0, X_STRIDES)) * COLORS + color
     hr_index = jnp.sum(is_here * jnp.where(is_used, hr_index, 2 * HALF)[None, :], axis=1)
-    first = (keys != jnp.concatenate([jnp.full((1,), -1, jnp.int32), keys[:-1]])).astype(jnp.int32)
     rows = jnp.arange(2 * HALF, dtype=jnp.int32)
     upto = jnp.sum((key[None, :] <= rows[:, None]).astype(jnp.int32), axis=1)
     has = jnp.any(key[None, :] == rows[:, None], axis=1)
@@ -543,8 +552,8 @@
             dma,
             dma((COLORS, 3)),
             dma((COLORS, 3)),
-            dma((COLORS, 2, 2)),
-            dma((COLORS, 2, 2)),
+            dma((COLORS, 2, 5)),
+            dma((COLORS, 2, 5)),
             dma((COLORS, 4, 2, 2)),
             dma((COLORS, 4, 2, 2)),
             dma((COLORS, 13)),
@@ -553,8 +562,8 @@
             dma((COLORS, 4, 4)),
             dma((COLORS, 4, 2, 2)),
             dma((COLORS, 4, 2, 2)),
-            dma((COLORS, 2, 2)),
-            dma((COLORS, 2, 2)),
+            dma((COLORS, 2, 5)),
+            dma((COLORS, 2, 5)),
             dma((COLORS, 3)),
             dma((COLORS, 3)),
             dma((4, 3)),
@@ -569,7 +578,7 @@
     )(
         order,
         xs,
-        first,
+        keys,
         hr_index,
         last,
         tile_values,

time: 211 us -> 201 us (0.953)
  Pallas kernels: 204 us -> 195 us
    pallas_call x1, Pallas kernels: 204 us -> 195 us  [shards(): pl.pallas_call(kernel, out_shape=(jax.ShapeDtypeStruct((TEMPS, COLORS * T...]
where the time goes in v5:
time: 201 us
  Pallas kernels  195 us (97%)
  local copies, waits for them, and re-layouts  2.72 us (1%)
  other arithmetic  2.57 us (1%)
    pallas_call x1, Pallas kernels, shards(): pl.pallas_call(kernel, out_shape=(jax.ShapeDtypeStruct((TEMPS, COLORS * T...  195 us

profile of v5, /device:TPU:0, one launch (start us, length us, event | category | flops | bytes accessed | tf_op | source)
XLA Modules:
  0.0 201.2 jit_solution(17922316777393199964)
XLA Ops:
  1.3 0.7 compare_select_fusion.16
  2.0 0.1 fusion
  2.2 0.2 convert_reduce_fusion.1
  2.4 0.8 select_reduce_fusion
  3.1 0.1 convert_reduce_fusion
  3.3 0.6 add_select_fusion.last_ref
  3.9 194.6 %solve.1 = (f32[64,384]{1,0:T(8,128)}, f32[1,128]{1,0:T(1,128)}) custom-call(s32[128]{0:T(128)} %get-tuple-element.9.order_ref, s32[128]{0:T(128)} %get-tuple-element.8.xs_ref, s32[128]{0:T(128)} %get-tuple-element.7.keys_ref, s32[128]{0:T(128)} %get-tuple-element.6.hr_index_ref, s32[384]{0:T(512)} %add_select_fusion.last_ref, f32[128,128,128]{2,1,0:T(8,128)} %tiles_hbm.1, ...), custom_call_target="tpu_custom_call" | custom-call | tf_op jit(solution)/shard_map/solve/pallas_call | solution.py:532
  198.5 1.2 slice_bitcast_fusion
  199.6 1.5 copy.12
  (1 shorter events, 0.0 us)

commit v6 on v5

--- a/solution.py
+++ b/solution.py
@@ -135,10 +135,10 @@
         sends.append(copy)
         return copy
 
-    def drain():
-        for copy in sends:
+    def drain(count):
+        for copy in sends[:count]:
             copy.wait_send()
-        sends.clear()
+        del sends[:count]
 
     def to(c, p, way):
         return at(ORDERS[c][p], 1 + 2 * way)
@@ -270,7 +270,6 @@
         first_only(sweep, lambda: receive(weights_to_mate()))
         for copy in forwards:
             copy.wait_recv()
-        drain()
 
     def multiply():
         unroll = 32
@@ -338,6 +337,7 @@
         pl.when(sweep == ITERS - 1)(act)
 
     def scatter(sweep):
+        gather_sends = len(sends)
         pair, half, full, tail, last = {}, {}, {}, {}, {}
 
         def yt(c, g, j):
@@ -467,8 +467,11 @@
         for k, (act, *group) in enumerate(plan):
             for c in everyone:
                 act(c, *group)
+            if k == 6:
+                drain(gather_sends)
             if k in (3, 7, 10):
                 last_only(sweep, lambda k=k: start_round((3, 7, 10).index(k)))
+        drain(len(sends) - 3 * COLORS)
         for c in everyone:
             for step in (1, 3, 2):
                 last[c, step].wait_recv()
@@ -477,7 +480,7 @@
             flux = relax(c) * (driving_ref[:, lanes(c)] + total)
             flux_ref[:, lanes(c)] = flux
             x_all[own[c]] = flux
-        drain()
+        drain(len(sends))
 
     def sweep_once(sweep, carry):
         gather(sweep)

time: 201 us -> 200 us (level)
  no operation moved by 1% of the time
where the time goes in v6:
time: 200 us
  Pallas kernels  193 us (96%)
  local copies, waits for them, and re-layouts  2.72 us (1%)
  other arithmetic  2.57 us (1%)
    pallas_call x1, Pallas kernels, shards(): pl.pallas_call(kernel, out_shape=(jax.ShapeDtypeStruct((TEMPS, COLORS * T...  193 us

profile of v6, /device:TPU:0, one launch (start us, length us, event | category | flops | bytes accessed | tf_op | source)
XLA Modules:
  0.0 199.9 jit_solution(12597494719479985852)
XLA Ops:
  1.3 0.7 compare_select_fusion.16
  2.0 0.1 fusion
  2.2 0.2 convert_reduce_fusion.1
  2.4 0.8 select_reduce_fusion
  3.1 0.1 convert_reduce_fusion
  3.3 0.6 add_select_fusion.last_ref
  3.9 193.3 %solve.1 = (f32[64,384]{1,0:T(8,128)}, f32[1,128]{1,0:T(1,128)}) custom-call(s32[128]{0:T(128)} %get-tuple-element.9.order_ref, s32[128]{0:T(128)} %get-tuple-element.8.xs_ref, s32[128]{0:T(128)} %get-tuple-element.7.keys_ref, s32[128]{0:T(128)} %get-tuple-element.6.hr_index_ref, s32[384]{0:T(512)} %add_select_fusion.last_ref, f32[128,128,128]{2,1,0:T(8,128)} %tiles_hbm.1, ...), custom_call_target="tpu_custom_call" | custom-call | tf_op jit(solution)/shard_map/solve/pallas_call | solution.py:535
  197.2 1.2 slice_bitcast_fusion
  198.4 1.5 copy.12
  (1 shorter events, 0.0 us)
